TPU v7x, 32 devices: a whole 2x2x4 slice. The times are simulated.
32 devices in a mesh: lat: 4 (over y, core), lon: 8 (over z, x).
Axes of the slice: x: 2, y: 2, z: 4, core: 2. Of those that a mesh axis runs over, the one named last changes fastest.
Arguments:
- queries: bfloat16 [12, 360, 1024], P('lat', 'lon'), may hold values from -68 to 68
- keys: bfloat16 [12, 360, 1024], P('lat', 'lon'), may hold values from -6 to 6
- values: bfloat16 [12, 360, 1024], P('lat', 'lon'), may hold values from -6 to 6
- cotangent: bfloat16 [12, 360, 1024], P('lat', 'lon'), may hold values from -6 to 6
- pair_list: int32 [12, 9], replicated, may hold values from -1 to 8, as said below
- quad_index: int32 [12], replicated, may hold values from 0 to 31
- quad_table: float32 [32], replicated, may hold values from 0.1 to 1
Outputs:
- attended: bfloat16 [12, 360, 1024], P('lat', 'lon')
- grad_queries: bfloat16 [12, 360, 1024], P('lat', 'lon')
- grad_keys: bfloat16 [12, 360, 1024], P('lat', 'lon')
- grad_values: bfloat16 [12, 360, 1024], P('lat', 'lon')
Inputs may be any that keep to these rules, and one draw needn't show every extreme that they name: `pair_list`: row r lists distinct codes in increasing order, then -1 in the remaining slots; code 4 (the query tile itself) is always listed, codes 1 and 7 are listed wherever the row they name lies inside 0 to 11, and no listed code names a row outside 0 to 11.
All inputs are finite; a program needn't handle non-finite values.
Results may differ from a plain program's by a relative error of at most 0.012.
The roundings to bfloat16 on the way count: a program that leaves them out, or rounds other values in their place, can miss the bound.
Values may be sent and summed in bfloat16 or wider, within the bound.
No kernel may reach another device: no remote copies, remote signals or barrier semaphores. Data moves between devices by JAX's collectives and lax.ppermute only.
A program may use at most 64 MiB of HBM per device.

v0:
```python
import functools
import jax
import jax.numpy as jnp
from jax import lax
from jax.experimental import pallas as pl
from jax.experimental.pallas import tpu as pltpu
from jax.sharding import Mesh, PartitionSpec as P

HEADS = 16
HEAD = 64
TILE = 45
NPAIR = 9
LANES = 128
SLOT = 48
HALF = 2 * SLOT
WIDTH = 2 * HALF
LON_GROUP = 2
CHUNKS = HEADS * HEAD // LANES
ROUTES = (5, 7, 4, 6, 1, 3, 2)
FAR = -1e30
FLIGHT = 3
GROUP = ("lat_in", "lon_in")


f32, bf16 = jnp.float32, jnp.bfloat16


def dot(a, b, da, db):
    return lax.dot_general(a, b, (((da,), (db,)), ((), ())), preferred_element_type=f32)


def pack_kernel(me_ref, first_ref, second_ref, *out_refs):
    me = me_ref[0]
    for o, out_ref in enumerate(out_refs):
        lanes = pl.ds(pl.multiple_of((me ^ o) * LANES, LANES), LANES)
        for kv, ref in enumerate((first_ref, second_ref)):
            for i in range(ref.shape[0]):
                out_ref[kv, i, 32:] = jnp.zeros((SLOT - 32, LANES), bf16)
                out_ref[kv, i, :TILE] = ref[i, :, lanes]


def unpack_kernel(me_ref, *refs):
    me = me_ref[0]
    outs = refs[CHUNKS:]
    for o, block_ref in enumerate(refs[:CHUNKS]):
        lanes = pl.ds(pl.multiple_of((me ^ o) * LANES, LANES), LANES)
        for kv, ref in enumerate(outs):
            for i in range(ref.shape[0]):
                ref[i, :, lanes] = block_ref[kv, i, :TILE]


def head_masks():
    low = lax.broadcasted_iota(jnp.int32, (SLOT, LANES), 1) < HEAD
    return low, low.astype(bf16), jnp.logical_not(low).astype(bf16)


def pad_rows():
    row = lax.broadcasted_iota(jnp.int32, (8, WIDTH), 0)
    return jnp.where(row < TILE - (SLOT - 8), 0.0, FAR)


def stacked(pair, masks):
    tall = [jnp.concatenate([t * masks[1], t * masks[2]], 0) for t in pair]
    blank = jnp.zeros((HALF, LANES), bf16)
    split = [
        jnp.concatenate([tall[0], blank], 1),
        jnp.concatenate([blank, tall[1]], 1),
    ]
    return jnp.concatenate(tall, 0), jnp.concatenate(split, 0)


def biased(scores, rows, pad):
    parts = []
    for j, row in enumerate(rows):
        block = scores[j * SLOT : (j + 1) * SLOT]
        parts += [block[: SLOT - 8] + row, block[SLOT - 8 :] + (row + pad)]
    return jnp.concatenate(parts, 0)


def interleaved(line, rows):
    flight = FLIGHT if rows % FLIGHT == 0 else 1

    def step(i, carry):
        waiting = [line(i * flight + k) for k in range(flight)]
        live = []
        while waiting or live:
            if waiting:
                live.append(waiting.pop(0))
            live = [one for one in live if next(one, FAR) != FAR]
        return carry

    lax.fori_loop(0, rows // flight, step, 0)


def main_kernel(rows, band_rows, me_ref, bias_ref, qg_ref, odd_ref, even_ref, cap_ref, *refs):
    block_refs = refs[:CHUNKS]
    out_ref, acc, ext, stat_ref = refs[CHUNKS:]
    me = me_ref[0]
    side = me & 1

    def place(tile_row, tile, value):
        for kv in range(2):
            ext[kv, tile_row + 1, tile] = value[kv]

    for o, ref in enumerate(block_refs):
        source = me ^ o
        for i in range(band_rows):
            place((source >> 1) * band_rows + i, 1 + (source & 1), ref[:, i])
    for j in range(CHUNKS // 2):
        for ref, o, tile in ((odd_ref, 2 * j + 1, 3 * side), (even_ref, 2 * j, 3 - 3 * side)):
            for i in range(band_rows):
                place(((me ^ o) >> 1) * band_rows + i, tile, ref[j, :, i])
    for end in range(2):
        for kv in range(2):
            ext[kv, end * (rows + 1)] = cap_ref[end, kv]
    acc[...] = jnp.zeros_like(acc)
    masks = head_masks()
    pad = pad_rows()

    def merge(full):
        tiles = []
        for x in range(2):
            part = full[x * HALF : (x + 1) * HALF, x * LANES : (x + 1) * LANES]
            tiles.append(jnp.where(masks[0], part[:SLOT], part[SLOT:]))
        return tiles

    def as_column(row):
        return jnp.transpose(jnp.broadcast_to(row, (8, WIDTH)))[:, :1]

    def gathered(kv, r):
        inside = jnp.concatenate([ext[kv, r + a, x] for a in range(3) for x in (1, 2)], 0)
        rim = jnp.concatenate(
            [jnp.concatenate([ext[kv, r + a, 0], ext[kv, r + a, 3]], 1) for a in range(3)], 0
        )
        return inside, rim, jnp.concatenate([jnp.concatenate([inside, inside], 1), rim], 0)

    def line(r):
        band, inner = r // band_rows, r % band_rows
        scale = jnp.asarray(HEAD**-0.5, bf16)
        q_two, q_split = stacked([qg_ref[band * 2 + x, 0, inner] * scale for x in range(2)], masks)
        g_two, g_split = stacked([qg_ref[band * 2 + x, 1, inner] for x in range(2)], masks)
        k_in, k_rim, k_all = gathered(0, r)
        v_in, v_rim, v_all = gathered(1, r)
        yield
        scores = jnp.concatenate([dot(k_in, q_two, 1, 1), dot(k_rim, q_split, 1, 1)], 0)
        grad_probs = jnp.concatenate([dot(v_in, g_two, 1, 1), dot(v_rim, g_split, 1, 1)], 0)
        yield
        shifted = biased(scores, [bias_ref[r, j : j + 1] for j in range(NPAIR)], pad)
        top = jnp.max(shifted, axis=0, keepdims=True)
        yield
        shares = jnp.exp(shifted - top)
        total = jnp.sum(shares, axis=0, keepdims=True)
        inverse = 1.0 / total
        yield
        mixed = dot(shares.astype(bf16), v_all, 0, 0)
        yield
        attended = [t.astype(bf16) for t in merge(mixed / as_column(total))]
        for x in range(2):
            out_ref[band * 2 + x, 0, inner] = attended[x]
        tall = jnp.concatenate([t.astype(f32) for t in attended for _ in range(2)], 0)
        products = g_two.astype(f32) * tall
        delta = jnp.sum(jnp.transpose(products), axis=0, keepdims=True)
        stat_ref[0, pl.ds(r, 1)] = top + jnp.log(total)
        stat_ref[1, pl.ds(r, 1)] = delta
        yield
        probs = shares * inverse
        slopes = (probs * (grad_probs - delta)).astype(bf16)
        probs = probs.astype(bf16)
        yield
        dq = merge(dot(slopes, k_all, 0, 0) * HEAD**-0.5)
        for x in range(2):
            out_ref[band * 2 + x, 1, inner] = dq[x].astype(bf16)
        yield
        for kv, left, two in ((0, slopes, q_two), (1, probs, g_two)):
            inside = dot(left[: 6 * SLOT], two, 1, 0)
            for a in range(3):
                for x in range(2):
                    at = (2 * a + x) * SLOT
                    acc[kv, r + a, x] += inside[at : at + SLOT]

    interleaved(line, rows)


def rim_kernel(rows, band_rows, me_ref, bias_ref, ext, sum_ref, west_ref, east_ref,
               west_stat, east_stat, *refs):
    block_refs = refs[:CHUNKS]
    cap_ref, acc = refs[CHUNKS:]
    me = me_ref[0]
    masks = head_masks()
    pad = pad_rows()
    from_east = lax.broadcasted_iota(jnp.int32, (1, WIDTH), 1) < HALF
    acc[...] = sum_ref[...]

    def line(r):
        band, inner = r // band_rows, r % band_rows
        scale = jnp.asarray(HEAD**-0.5, bf16)
        q_split = stacked([ref[band, 0, inner] * scale for ref in (east_ref, west_ref)], masks)[1]
        g_split = stacked([ref[band, 1, inner] for ref in (east_ref, west_ref)], masks)[1]
        k_own, v_own = [
            jnp.concatenate(
                [jnp.concatenate([ext[kv, r + a, 2], ext[kv, r + a, 1]], 1) for a in range(3)], 0
            )
            for kv in range(2)
        ]
        lse, delta = [
            jnp.where(from_east, east_stat[s, pl.ds(r, 1)], west_stat[s, pl.ds(r, 1)])
            for s in range(2)
        ]
        yield
        scores = dot(k_own, q_split, 1, 1)
        grad_probs = dot(v_own, g_split, 1, 1)
        yield
        shifted = biased(scores, [bias_ref[r, j : j + 1] for j in range(6, NPAIR)], pad)
        probs = jnp.exp(shifted - lse)
        slopes = (probs * (grad_probs - delta)).astype(bf16)
        probs = probs.astype(bf16)
        yield
        for kv, left, split in ((0, slopes, q_split), (1, probs, g_split)):
            part = dot(left, split, 1, 0)
            for a in range(3):
                acc[kv, r + a, 1] += part[a * SLOT : (a + 1) * SLOT, :LANES]
                acc[kv, r + a, 0] += part[a * SLOT : (a + 1) * SLOT, LANES:]

    interleaved(line, rows)
    for o, ref in enumerate(block_refs):
        target = me ^ o
        for kv in range(2):
            for i in range(band_rows):
                row = (target >> 1) * band_rows + i + 1
                ref[kv, i] = acc[kv, row, target & 1].astype(bf16)
    for end in range(2):
        for kv in range(2):
            cap_ref[end, kv] = acc[kv, end * (rows + 1)].astype(bf16)


def shift(value, axis, by, wrap):
    size = lax.axis_size(axis)
    pairs = [(i, (i + by) % size) for i in range(size) if wrap or 0 <= i + by < size]
    return lax.ppermute(value, axis, pairs)


def crossed(value, by):
    count, inner = lax.axis_size("lon_out"), lax.axis_size("lon_in")
    pairs = []
    for z in range(count):
        for x in range(inner):
            there = (z + (by if x == 0 else -by)) % count
            pairs.append((z * inner + x, there * inner + x))
    return lax.ppermute(value, ("lon_out", "lon_in"), pairs)


def swapped(blocks):
    out = [None] * CHUNKS
    out[0] = blocks[0]
    for o in ROUTES:
        out[o] = lax.ppermute(blocks[o], GROUP, [(i, i ^ o) for i in range(CHUNKS)])
    return out


def packed(first, second):
    both = jnp.stack([first, second])
    both = jnp.pad(both, ((0, 0), (0, 0), (0, SLOT - TILE), (0, 0)))
    split = both.reshape(both.shape[:3] + (both.shape[3] // LANES, LANES))
    return split.transpose(3, 0, 1, 2, 4)


def unpacked(block):
    moved = block.transpose(1, 2, 3, 0, 4)
    joined = moved.reshape(moved.shape[:3] + (moved.shape[3] * LANES,))
    return joined[:, :, :TILE]


def bias_table(pair_list, quad_index, quad_table, first_row, rows):
    lat_count = pair_list.shape[0]
    own_row = first_row + jnp.arange(rows, dtype=jnp.int32)
    code = jnp.arange(NPAIR, dtype=jnp.int32)
    if lat_count > rows:
        pairs = lax.dynamic_slice_in_dim(pair_list, first_row, rows, 0)
    else:
        pairs = pair_list
    listed = jnp.any(pairs[:, :, None] == code, axis=1)
    source = own_row[:, None] + code // 3 - 1
    pick = source[..., None] == jnp.arange(lat_count, dtype=jnp.int32)
    entry = jnp.sum(jnp.where(pick, quad_index, 0), axis=2)
    pick = entry[..., None] == jnp.arange(quad_table.shape[0], dtype=jnp.int32)
    weight = jnp.sum(jnp.where(pick, quad_table, 0.0), axis=2)
    bias = jnp.where(listed, jnp.log(weight), FAR).reshape(rows, 3, 3)
    first = jnp.concatenate([bias[:, :, 1:].reshape(rows, 6), bias[:, :, 0]], 1)
    second = jnp.concatenate([bias[:, :, :2].reshape(rows, 6), bias[:, :, 2]], 1)
    lane = jnp.arange(WIDTH, dtype=jnp.int32)
    return jnp.where(lane < HALF, first[:, :, None], second[:, :, None])


def on_device(queries, keys, values, cotangent, pair_list, quad_index, quad_table):
    band_rows = queries.shape[0]
    bands = lax.axis_size("lat_in")
    rows = band_rows * bands
    lat_groups = lax.axis_size("lat_out")
    me = lax.axis_index(GROUP).astype(jnp.int32)
    me_list = me.reshape(1)
    smem = pl.BlockSpec(memory_space=pltpu.SMEM)
    vmem = pl.BlockSpec(memory_space=pltpu.VMEM)
    params = pltpu.CompilerParams(vmem_limit_bytes=32 * 2**20)
    block = jax.ShapeDtypeStruct((2, band_rows, SLOT, LANES), bf16)
    natural = jnp.arange(CHUNKS, dtype=jnp.int32) ^ me

    def exchange(value):
        return lax.all_to_all(value, GROUP, 0, 0, tiled=True)

    def halves(value):
        return value.reshape((bands, 2) + value.shape[1:])

    blocks = pl.pallas_call(
        pack_kernel,
        out_shape=(block,) * CHUNKS,
        in_specs=[smem, vmem, vmem],
        out_specs=(vmem,) * CHUNKS,
        compiler_params=params,
        name="pack_keys",
    )(me_list, keys, values)
    blocks = swapped(blocks)
    odd = crossed(jnp.stack(blocks[1::2]), 1)
    even = crossed(jnp.stack(blocks[0::2]), -1)
    qg = exchange(packed(queries, cotangent))
    west = shift(halves(qg)[:, 1], "lon_out", 1, True)
    east = shift(halves(qg)[:, 0], "lon_out", -1, True)
    if lat_groups > 1:
        whole = halves(jnp.stack(blocks)[natural])
        spot = natural[::2] // 2
        odd_n, even_n = odd[spot], even[spot]
        left = jnp.where(me % 2 == 0, odd_n, even_n)
        right = jnp.where(me % 2 == 0, even_n, odd_n)

        def edge(band, inner):
            tiles = [left[band, :, inner], whole[band, 0, :, inner],
                     whole[band, 1, :, inner], right[band, :, inner]]
            return jnp.stack(tiles, 1)

        north = shift(edge(bands - 1, band_rows - 1), "lat_out", 1, False)
        south = shift(edge(0, 0), "lat_out", -1, False)
        caps = jnp.stack([north, south])
        first_row = (lax.axis_index("lat_out") * rows).astype(jnp.int32)
    else:
        caps = jnp.zeros((2, 2, 4, SLOT, LANES), bf16)
        first_row = 0
    bias = bias_table(pair_list, quad_index, quad_table, first_row, rows)
    out, acc, ext, stats = pl.pallas_call(
        functools.partial(main_kernel, rows, band_rows),
        out_shape=(
            jax.ShapeDtypeStruct(qg.shape, bf16),
            jax.ShapeDtypeStruct((2, rows + 2, 2, SLOT, LANES), f32),
            jax.ShapeDtypeStruct((2, rows + 2, 4, SLOT, LANES), bf16),
            jax.ShapeDtypeStruct((2, rows, WIDTH), f32),
        ),
        in_specs=[smem] + [vmem] * (5 + CHUNKS),
        out_specs=(vmem,) * 4,
        compiler_params=params,
        name="main_rows",
    )(me_list, bias, qg, odd, even, caps, *blocks)
    west_stat = shift(stats, "lon_out", 1, True)
    east_stat = shift(stats, "lon_out", -1, True)
    out = exchange(out)
    grads = pl.pallas_call(
        functools.partial(rim_kernel, rows, band_rows),
        out_shape=(block,) * CHUNKS
        + (jax.ShapeDtypeStruct((2, 2, 2, SLOT, LANES), bf16),),
        in_specs=[smem] + [vmem] * 7,
        out_specs=(vmem,) * (CHUNKS + 1),
        scratch_shapes=[pltpu.VMEM(acc.shape, f32)],
        compiler_params=params,
        name="rim_rows",
    )(me_list, bias, ext, acc, west, east, west_stat, east_stat)
    blocks, cap = grads[:CHUNKS], grads[CHUNKS]
    if lat_groups > 1:
        north = shift(cap[1], "lat_out", 1, False).astype(f32)
        south = shift(cap[0], "lat_out", -1, False).astype(f32)
        whole = halves(jnp.stack(blocks)[natural]).astype(f32)
        for band, inner, add in ((0, 0, north), (bands - 1, band_rows - 1, south)):
            whole = whole.at[band, :, :, inner].add(add.swapaxes(0, 1))
        whole = whole.astype(bf16).reshape((CHUNKS,) + block.shape)[natural]
        blocks = [whole[o] for o in range(CHUNKS)]
    blocks = swapped(blocks)
    tile = jax.ShapeDtypeStruct(queries.shape, bf16)
    dk, dv = pl.pallas_call(
        unpack_kernel,
        out_shape=(tile, tile),
        in_specs=[smem] + [vmem] * CHUNKS,
        out_specs=(vmem, vmem),
        compiler_params=params,
        name="unpack_grads",
    )(me_list, *blocks)
    out = unpacked(out)
    return out[0], out[1], dk, dv


def solution(mesh):
    lat, lon = mesh.shape["lat"], mesh.shape["lon"]
    lon_in = LON_GROUP
    lat_in = CHUNKS // lon_in
    finer = Mesh(
        mesh.devices.reshape(lat // lat_in, lat_in, lon // lon_in, lon_in),
        ("lat_out", "lat_in", "lon_out", "lon_in"),
    )
    spec = P(("lat_out", "lat_in"), ("lon_out", "lon_in"), None)
    return jax.shard_map(
        on_device,
        mesh=finer,
        in_specs=(spec,) * 4 + (P(),) * 3,
        out_specs=(spec,) * 4,
        check_vma=False,
    )
```

profile of v0, /device:TPU:1, one launch (start us, length us, event | category | flops | bytes accessed | tf_op | source)
XLA Modules:
  0.0 97.4 jit_solution(2626739309271507057)
XLA Ops:
  2.7 2.1 %collective-permute-start.6 = (bf16[2,3,48,128]{3,2,1,0:T(8,128)(2,1)S(1)}, bf16[2,3,48,128]{3,2,1,0:T(8,128)(2,1)S(1)}, u32[]{:S(2)}, u32[]{:S(2)}) collective-permute-start(bf16[2,3,48,128]{3,2,1,0:T(8,128)(2,1)S(1)} %get-tuple-element.32), channel_id=1, source_target_pairs={{0,16},{1,17},{8,24},{9,25},{16,0},{17,1},{24,8},{25,9},{2,18},{3,... | collective-permute-start | bytes 221192 | tf_op jit(solution)/shard_map/ppermute | solution.py:256
  5.8 1.3 %collective-permute-start = (bf16[2,3,48,128]{3,2,1,0:T(8,128)(2,1)S(1)}, bf16[2,3,48,128]{3,2,1,0:T(8,128)(2,1)S(1)}, u32[]{:S(2)}, u32[]{:S(2)}) collective-permute-start(bf16[2,3,48,128]{3,2,1,0:T(8,128)(2,1)S(1)} %get-tuple-element.26), channel_id=1, source_target_pairs={{0,1},{1,0},{8,9},{9,8},{16,17},{17,16},{24,25},{25,24},{2,3},{3,2... | collective-permute-start | bytes 221192 | tf_op jit(solution)/shard_map/ppermute | solution.py:256
  7.7 2.0 %bitcast_bitcast_fusion = bf16[8,2,3,48,128]{4,3,2,1,0:T(8,128)(2,1)} fusion(bf16[1,3,45,1024]{3,2,1,0:T(8,128)(2,1)} %bitcast.56, bf16[1,3,45,1024]{3,2,1,0:T(8,128)(2,1)} %bitcast.57), kind=kLoop, calls=%fused_computation.6 | loop fusion | flops 2064384 | bytes 1142784 | tf_op jit(solution)/shard_map/transpose | solution.py:264
  9.7 4.3 %all-to-all-start = ((bf16[8,2,3,48,128]{4,3,2,1,0:T(8,128)(2,1)}), bf16[8,2,3,48,128]{4,3,2,1,0:T(8,128)(2,1)S(1)}, u32[]{:S(2)}, u32[]{:S(2)}) async-start(bf16[8,2,3,48,128]{4,3,2,1,0:T(8,128)(2,1)} %bitcast_bitcast_fusion), calls=%async_computation | async-start | bytes 1179648 | tf_op jit(solution)/shard_map/all_to_all | solution.py:308
  15.2 2.3 %collective-permute-start.2 = (bf16[2,3,48,128]{3,2,1,0:T(8,128)(2,1)S(1)}, bf16[2,3,48,128]{3,2,1,0:T(8,128)(2,1)S(1)}, u32[]{:S(2)}, u32[]{:S(2)}) collective-permute-start(bf16[2,3,48,128]{3,2,1,0:T(8,128)(2,1)S(1)} %get-tuple-element.28), channel_id=1, source_target_pairs={{0,17},{1,16},{8,25},{9,24},{16,1},{17,0},{24,9},{25,8},{2,19},{3,... | collective-permute-start | bytes 221192 | tf_op jit(solution)/shard_map/ppermute | solution.py:256
  18.0 3.4 %collective-permute-start.8 = (bf16[4,2,3,48,128]{4,3,2,1,0:T(8,128)(2,1)S(1)}, bf16[4,2,3,48,128]{4,3,2,1,0:T(8,128)(2,1)S(1)}, u32[]{:S(2)}, u32[]{:S(2)}) collective-permute-start(bf16[4,2,3,48,128]{4,3,2,1,0:T(8,128)(2,1)S(1)} %pad_maximum_fusion.1), channel_id=1, source_target_pairs={{0,6},{1,3},{2,0},{3,5},{4,2},{5,7},{6,4},{7,1},{8,14},{9,11},{10,... | collective-permute-start | bytes 884744 | tf_op jit(solution)/shard_map/ppermute | solution.py:249
  21.4 3.6 %collective-permute-done.2.refs_5_ = bf16[2,3,48,128]{3,2,1,0:T(8,128)(2,1)S(1)} collective-permute-done((bf16[2,3,48,128]{3,2,1,0:T(8,128)(2,1)S(1)}, bf16[2,3,48,128]{3,2,1,0:T(8,128)(2,1)S(1)}, u32[]{:S(2)}, u32[]{:S(2)}) %collective-permute-start.2) | collective-permute-done | bytes 73760 | tf_op jit(solution)/shard_map/ppermute | solution.py:256
  25.0 1.9 %collective-permute-done.3.refs_7_ = bf16[2,3,48,128]{3,2,1,0:T(8,128)(2,1)S(1)} collective-permute-done((bf16[2,3,48,128]{3,2,1,0:T(8,128)(2,1)S(1)}, bf16[2,3,48,128]{3,2,1,0:T(8,128)(2,1)S(1)}, u32[]{:S(2)}, u32[]{:S(2)}) %collective-permute-start.3) | collective-permute-done | bytes 73760 | tf_op jit(solution)/shard_map/ppermute | solution.py:256
  26.9 1.3 %collective-permute-start.4 = (bf16[4,2,3,48,128]{4,3,2,1,0:T(8,128)(2,1)S(1)}, bf16[4,2,3,48,128]{4,3,2,1,0:T(8,128)(2,1)S(1)}, u32[]{:S(2)}, u32[]{:S(2)}) collective-permute-start(bf16[4,2,3,48,128]{4,3,2,1,0:T(8,128)(2,1)S(1)} %pad_maximum_fusion), channel_id=1, source_target_pairs={{0,2},{1,7},{2,4},{3,1},{4,6},{5,3},{6,0},{7,5},{8,10},{9,15},{10,... | collective-permute-start | bytes 884744 | tf_op jit(solution)/shard_map/ppermute | solution.py:249
  29.1 8.8 %collective-permute-done.4.odd_ref = bf16[4,2,3,48,128]{4,3,2,1,0:T(8,128)(2,1)S(1)} collective-permute-done((bf16[4,2,3,48,128]{4,3,2,1,0:T(8,128)(2,1)S(1)}, bf16[4,2,3,48,128]{4,3,2,1,0:T(8,128)(2,1)S(1)}, u32[]{:S(2)}, u32[]{:S(2)}) %collective-permute-start.4) | collective-permute-done | bytes 294944 | tf_op jit(solution)/shard_map/ppermute | solution.py:249
  47.7 8.5 %main_rows.1 = (bf16[8,2,3,48,128]{4,3,2,1,0:T(8,128)(2,1)S(1)}, f32[2,14,2,48,128]{4,3,2,1,0:T(8,128)S(1)}, bf16[2,14,4,48,128]{4,3,2,1,0:T(8,128)(2,1)S(1)}, f32[2,12,192]{2,1,0:T(8,128)S(1)}) custom-call(s32[1]{0:T(128)} %bitcast.me_ref, f32[12,9,192]{2,1,0:T(8,128)S(1)} %broadcast_select_fusion.bias_ref, ...), custom_call_target="tpu_custom_call" | custom-call | tf_op jit(solution)/shard_map/main_rows/pallas_call | solution.py:347
  57.6 4.7 %all-to-all-start.1 = ((bf16[8,2,3,48,128]{4,3,2,1,0:T(8,128)(2,1)}), bf16[8,2,3,48,128]{4,3,2,1,0:T(8,128)(2,1)}, u32[]{:S(2)}, u32[]{:S(2)}) async-start(bf16[8,2,3,48,128]{4,3,2,1,0:T(8,128)(2,1)} %copy-done), calls=%async_computation.1 | async-start | bytes 1179648 | tf_op jit(solution)/shard_map/all_to_all | solution.py:308
  62.3 1.5 %collective-permute-start.10 = (bf16[4,2,3,48,128]{4,3,2,1,0:T(8,128)(2,1)S(1)}, bf16[4,2,3,48,128]{4,3,2,1,0:T(8,128)(2,1)S(1)}, u32[]{:S(2)}, u32[]{:S(2)}) collective-permute-start(bf16[4,2,3,48,128]{4,3,2,1,0:T(8,128)(2,1)S(1)} %get-tuple-element.48), channel_id=1, source_target_pairs={{0,6},{2,0},{4,2},{6,4},{1,7},{3,1},{5,3},{7,5},{8,14},{10,8},{12,... | collective-permute-start | bytes 884744 | tf_op jit(solution)/shard_map/ppermute | solution.py:239
  63.9 3.3 %collective-permute-start.12 = (f32[2,12,192]{2,1,0:T(8,128)S(1)}, f32[2,12,192]{2,1,0:T(8,128)S(1)}, u32[]{:S(2)}, u32[]{:S(2)}) collective-permute-start(f32[2,12,192]{2,1,0:T(8,128)S(1)} %copy-done.24), channel_id=1, source_target_pairs={{0,6},{2,0},{4,2},{6,4},{1,7},{3,1},{5,3},{7,5},{8,14},{10,8},{12,... | collective-permute-start | bytes 55304 | tf_op jit(solution)/shard_map/ppermute | solution.py:239
  67.1 10.8 %collective-permute-done.11.west_stat = f32[2,12,192]{2,1,0:T(8,128)S(1)} collective-permute-done((f32[2,12,192]{2,1,0:T(8,128)S(1)}, f32[2,12,192]{2,1,0:T(8,128)S(1)}, u32[]{:S(2)}, u32[]{:S(2)}) %collective-permute-start.11) | collective-permute-done | bytes 18464 | tf_op jit(solution)/shard_map/ppermute | solution.py:239
  78.0 3.1 %rim_rows.1 = (bf16[2,3,48,128]{3,2,1,0:T(8,128)(2,1)S(1)}, bf16[2,3,48,128]{3,2,1,0:T(8,128)(2,1)S(1)}, bf16[2,3,48,128]{3,2,1,0:T(8,128)(2,1)S(1)}, bf16[2,3,4...) custom-call(s32[1]{0:T(128)} %bitcast.me_ref, ...), custom_call_target="tpu_custom_call" | custom-call | tf_op jit(solution)/shard_map/rim_rows/pallas_call | solution.py:363
  81.0 1.1 %collective-permute-start.13 = (bf16[2,3,48,128]{3,2,1,0:T(8,128)(2,1)S(1)}, bf16[2,3,48,128]{3,2,1,0:T(8,128)(2,1)S(1)}, u32[]{:S(2)}, u32[]{:S(2)}) collective-permute-start(bf16[2,3,48,128]{3,2,1,0:T(8,128)(2,1)S(1)} %get-tuple-element.39), channel_id=1, source_target_pairs={{0,1},{1,0},{8,9},{9,8},{16,17},{17,16},{24,25},{25,24},{2,3},{3,2... | collective-permute-start | bytes 221192 | tf_op jit(solution)/shard_map/ppermute | solution.py:256
  82.1 2.1 %collective-permute-start.14 = (bf16[2,3,48,128]{3,2,1,0:T(8,128)(2,1)S(1)}, bf16[2,3,48,128]{3,2,1,0:T(8,128)(2,1)S(1)}, u32[]{:S(2)}, u32[]{:S(2)}) collective-permute-start(bf16[2,3,48,128]{3,2,1,0:T(8,128)(2,1)S(1)} %get-tuple-element.40), channel_id=1, source_target_pairs={{0,8},{1,9},{8,0},{9,1},{16,24},{17,25},{24,16},{25,17},{2,10},{3,... | collective-permute-start | bytes 221192 | tf_op jit(solution)/shard_map/ppermute | solution.py:256
  84.2 1.4 %collective-permute-start.16 = (bf16[2,3,48,128]{3,2,1,0:T(8,128)(2,1)S(1)}, bf16[2,3,48,128]{3,2,1,0:T(8,128)(2,1)S(1)}, u32[]{:S(2)}, u32[]{:S(2)}) collective-permute-start(bf16[2,3,48,128]{3,2,1,0:T(8,128)(2,1)S(1)} %get-tuple-element.42), channel_id=1, source_target_pairs={{0,16},{1,17},{8,24},{9,25},{16,0},{17,1},{24,8},{25,9},{2,18},{3,... | collective-permute-start | bytes 221192 | tf_op jit(solution)/shard_map/ppermute | solution.py:256
  85.6 1.2 %collective-permute-start.17 = (bf16[2,3,48,128]{3,2,1,0:T(8,128)(2,1)S(1)}, bf16[2,3,48,128]{3,2,1,0:T(8,128)(2,1)S(1)}, u32[]{:S(2)}, u32[]{:S(2)}) collective-permute-start(bf16[2,3,48,128]{3,2,1,0:T(8,128)(2,1)S(1)} %get-tuple-element.43), channel_id=1, source_target_pairs={{0,17},{1,16},{8,25},{9,24},{16,1},{17,0},{24,9},{25,8},{2,19},{3,... | collective-permute-start | bytes 221192 | tf_op jit(solution)/shard_map/ppermute | solution.py:256
  86.8 2.2 %collective-permute-start.18 = (bf16[2,3,48,128]{3,2,1,0:T(8,128)(2,1)S(1)}, bf16[2,3,48,128]{3,2,1,0:T(8,128)(2,1)S(1)}, u32[]{:S(2)}, u32[]{:S(2)}) collective-permute-start(bf16[2,3,48,128]{3,2,1,0:T(8,128)(2,1)S(1)} %get-tuple-element.44), channel_id=1, source_target_pairs={{0,24},{1,25},{8,16},{9,17},{16,8},{17,9},{24,0},{25,1},{2,26},{3,... | collective-permute-start | bytes 221192 | tf_op jit(solution)/shard_map/ppermute | solution.py:256
  89.9 4.4 %collective-permute-done.18.refs_6_ = bf16[2,3,48,128]{3,2,1,0:T(8,128)(2,1)S(1)} collective-permute-done((bf16[2,3,48,128]{3,2,1,0:T(8,128)(2,1)S(1)}, bf16[2,3,48,128]{3,2,1,0:T(8,128)(2,1)S(1)}, u32[]{:S(2)}, u32[]{:S(2)}) %collective-permute-start.18) | collective-permute-done | bytes 73760 | tf_op jit(solution)/shard_map/ppermute | solution.py:256
  94.4 1.0 %unpack_grads.1 = (bf16[3,45,1024]{2,1,0:T(8,128)(2,1)}, bf16[3,45,1024]{2,1,0:T(8,128)(2,1)}) custom-call(s32[1]{0:T(128)} %bitcast.me_ref, bf16[2,3,48,128]{3,2,1,0:T(8,128)(2,1)S(1)} %get-tuple-element.38.refs_0_, bf16[2,3,48,128]{3,2,1,0:T(8,128)(2,1)S(1)} %collective-permute-done.13.refs_1_, ...), custom_call_target="tpu_custom_call" | custom-call | tf_op jit(solution)/shard_map/unpack_grads/pallas_call | solution.py:384
  95.3 1.1 %copy_bitcast_fusion = bf16[2,3,48,1024]{3,2,1,0:T(8,128)(2,1)S(1)} fusion(bf16[8,2,3,48,128]{4,3,2,1,0:T(8,128)(2,1)} %all-to-all-done.1), kind=kLoop, calls=%fused_computation.5 | loop fusion | bytes 1179648 | tf_op jit(solution)/shard_map/reshape | solution.py:269
  (108 shorter events, 19.2 us)
Async XLA Ops:
  2.7 12.5 %collective-permute-start.6 = (bf16[2,3,48,128]{3,2,1,0:T(8,128)(2,1)S(1)}, bf16[2,3,48,128]{3,2,1,0:T(8,128)(2,1)S(1)}, u32[]{:S(2)}, u32[]{:S(2)}) collective-permute-start(bf16[2,3,48,128]{3,2,1,0:T(8,128)(2,1)S(1)} %get-tuple-element.32), channel_id=1, source_target_pairs={{0,16},{1,17},{8,24},{9,25},{16,0},{17,1},{24,8},{25,9},{2,18},{3,... | collective-permute-start | bytes 221192 | tf_op jit(solution)/shard_map/ppermute | solution.py:256
  4.9 12.7 %collective-permute-start.7 = (bf16[2,3,48,128]{3,2,1,0:T(8,128)(2,1)S(1)}, bf16[2,3,48,128]{3,2,1,0:T(8,128)(2,1)S(1)}, u32[]{:S(2)}, u32[]{:S(2)}) collective-permute-start(bf16[2,3,48,128]{3,2,1,0:T(8,128)(2,1)S(1)} %get-tuple-element.33), channel_id=1, source_target_pairs={{0,24},{1,25},{8,16},{9,17},{16,8},{17,9},{24,0},{25,1},{2,26},{3,... | collective-permute-start | bytes 221192 | tf_op jit(solution)/shard_map/ppermute | solution.py:256
  5.5 12.4 %collective-permute-start.5 = (bf16[2,3,48,128]{3,2,1,0:T(8,128)(2,1)S(1)}, bf16[2,3,48,128]{3,2,1,0:T(8,128)(2,1)S(1)}, u32[]{:S(2)}, u32[]{:S(2)}) collective-permute-start(bf16[2,3,48,128]{3,2,1,0:T(8,128)(2,1)S(1)} %get-tuple-element.31), channel_id=1, source_target_pairs={{0,8},{1,9},{8,0},{9,1},{16,24},{17,25},{24,16},{25,17},{2,10},{3,... | collective-permute-start | bytes 221192 | tf_op jit(solution)/shard_map/ppermute | solution.py:256
  5.8 15.5 %collective-permute-start = (bf16[2,3,48,128]{3,2,1,0:T(8,128)(2,1)S(1)}, bf16[2,3,48,128]{3,2,1,0:T(8,128)(2,1)S(1)}, u32[]{:S(2)}, u32[]{:S(2)}) collective-permute-start(bf16[2,3,48,128]{3,2,1,0:T(8,128)(2,1)S(1)} %get-tuple-element.26), channel_id=1, source_target_pairs={{0,1},{1,0},{8,9},{9,8},{16,17},{17,16},{24,25},{25,24},{2,3},{3,2... | collective-permute-start | bytes 221192 | tf_op jit(solution)/shard_map/ppermute | solution.py:256
  7.1 14.2 %collective-permute-start.1 = (bf16[2,3,48,128]{3,2,1,0:T(8,128)(2,1)S(1)}, bf16[2,3,48,128]{3,2,1,0:T(8,128)(2,1)S(1)}, u32[]{:S(2)}, u32[]{:S(2)}) collective-permute-start(bf16[2,3,48,128]{3,2,1,0:T(8,128)(2,1)S(1)} %get-tuple-element.27), channel_id=1, source_target_pairs={{0,9},{1,8},{8,1},{9,0},{16,25},{17,24},{24,17},{25,16},{2,11},{3,... | collective-permute-start | bytes 221192 | tf_op jit(solution)/shard_map/ppermute | solution.py:256
  9.7 28.9 %all-to-all-start = ((bf16[8,2,3,48,128]{4,3,2,1,0:T(8,128)(2,1)}), bf16[8,2,3,48,128]{4,3,2,1,0:T(8,128)(2,1)S(1)}, u32[]{:S(2)}, u32[]{:S(2)}) async-start(bf16[8,2,3,48,128]{4,3,2,1,0:T(8,128)(2,1)} %bitcast_bitcast_fusion), calls=%async_computation | async-start | bytes 1179648 | tf_op jit(solution)/shard_map/all_to_all | solution.py:308
  15.2 9.8 %collective-permute-start.2 = (bf16[2,3,48,128]{3,2,1,0:T(8,128)(2,1)S(1)}, bf16[2,3,48,128]{3,2,1,0:T(8,128)(2,1)S(1)}, u32[]{:S(2)}, u32[]{:S(2)}) collective-permute-start(bf16[2,3,48,128]{3,2,1,0:T(8,128)(2,1)S(1)} %get-tuple-element.28), channel_id=1, source_target_pairs={{0,17},{1,16},{8,25},{9,24},{16,1},{17,0},{24,9},{25,8},{2,19},{3,... | collective-permute-start | bytes 221192 | tf_op jit(solution)/shard_map/ppermute | solution.py:256
  17.5 9.3 %collective-permute-start.3 = (bf16[2,3,48,128]{3,2,1,0:T(8,128)(2,1)S(1)}, bf16[2,3,48,128]{3,2,1,0:T(8,128)(2,1)S(1)}, u32[]{:S(2)}, u32[]{:S(2)}) collective-permute-start(bf16[2,3,48,128]{3,2,1,0:T(8,128)(2,1)S(1)} %get-tuple-element.29), channel_id=1, source_target_pairs={{0,25},{1,24},{8,17},{9,16},{16,9},{17,8},{24,1},{25,0},{2,27},{3,... | collective-permute-start | bytes 221192 | tf_op jit(solution)/shard_map/ppermute | solution.py:256
  17.9 20.7 %copy-start.11 = (bf16[2,3,48,128]{3,2,1,0:T(8,128)(2,1)}, bf16[2,3,48,128]{3,2,1,0:T(8,128)(2,1)S(1)}, u32[]{:S(2)}) copy-start(bf16[2,3,48,128]{3,2,1,0:T(8,128)(2,1)S(1)} %collective-permute-done.5.refs_2_) | copy-start | bytes 221188
  18.0 10.4 %collective-permute-start.8 = (bf16[4,2,3,48,128]{4,3,2,1,0:T(8,128)(2,1)S(1)}, bf16[4,2,3,48,128]{4,3,2,1,0:T(8,128)(2,1)S(1)}, u32[]{:S(2)}, u32[]{:S(2)}) collective-permute-start(bf16[4,2,3,48,128]{4,3,2,1,0:T(8,128)(2,1)S(1)} %pad_maximum_fusion.1), channel_id=1, source_target_pairs={{0,6},{1,3},{2,0},{3,5},{4,2},{5,7},{6,4},{7,1},{8,14},{9,11},{10,... | collective-permute-start | bytes 884744 | tf_op jit(solution)/shard_map/ppermute | solution.py:249
  21.3 17.3 %copy-start.13 = (bf16[2,3,48,128]{3,2,1,0:T(8,128)(2,1)}, bf16[2,3,48,128]{3,2,1,0:T(8,128)(2,1)S(1)}, u32[]{:S(2)}) copy-start(bf16[2,3,48,128]{3,2,1,0:T(8,128)(2,1)S(1)} %collective-permute-done.refs_1_) | copy-start | bytes 221188
  26.9 11.0 %collective-permute-start.4 = (bf16[4,2,3,48,128]{4,3,2,1,0:T(8,128)(2,1)S(1)}, bf16[4,2,3,48,128]{4,3,2,1,0:T(8,128)(2,1)S(1)}, u32[]{:S(2)}, u32[]{:S(2)}) collective-permute-start(bf16[4,2,3,48,128]{4,3,2,1,0:T(8,128)(2,1)S(1)} %pad_maximum_fusion), channel_id=1, source_target_pairs={{0,2},{1,7},{2,4},{3,1},{4,6},{5,3},{6,0},{7,5},{8,10},{9,15},{10,... | collective-permute-start | bytes 884744 | tf_op jit(solution)/shard_map/ppermute | solution.py:249
  57.6 37.8 %all-to-all-start.1 = ((bf16[8,2,3,48,128]{4,3,2,1,0:T(8,128)(2,1)}), bf16[8,2,3,48,128]{4,3,2,1,0:T(8,128)(2,1)}, u32[]{:S(2)}, u32[]{:S(2)}) async-start(bf16[8,2,3,48,128]{4,3,2,1,0:T(8,128)(2,1)} %copy-done), calls=%async_computation.1 | async-start | bytes 1179648 | tf_op jit(solution)/shard_map/all_to_all | solution.py:308
  62.3 15.6 %collective-permute-start.10 = (bf16[4,2,3,48,128]{4,3,2,1,0:T(8,128)(2,1)S(1)}, bf16[4,2,3,48,128]{4,3,2,1,0:T(8,128)(2,1)S(1)}, u32[]{:S(2)}, u32[]{:S(2)}) collective-permute-start(bf16[4,2,3,48,128]{4,3,2,1,0:T(8,128)(2,1)S(1)} %get-tuple-element.48), channel_id=1, source_target_pairs={{0,6},{2,0},{4,2},{6,4},{1,7},{3,1},{5,3},{7,5},{8,14},{10,8},{12,... | collective-permute-start | bytes 884744 | tf_op jit(solution)/shard_map/ppermute | solution.py:239
  63.8 14.1 %collective-permute-start.9 = (bf16[4,2,3,48,128]{4,3,2,1,0:T(8,128)(2,1)S(1)}, bf16[4,2,3,48,128]{4,3,2,1,0:T(8,128)(2,1)S(1)}, u32[]{:S(2)}, u32[]{:S(2)}) collective-permute-start(bf16[4,2,3,48,128]{4,3,2,1,0:T(8,128)(2,1)S(1)} %get-tuple-element.49), channel_id=1, source_target_pairs={{0,2},{2,4},{4,6},{6,0},{1,3},{3,5},{5,7},{7,1},{8,10},{10,12},{12... | collective-permute-start | bytes 884744 | tf_op jit(solution)/shard_map/ppermute | solution.py:239
  63.8 14.1 %collective-permute-start.11 = (f32[2,12,192]{2,1,0:T(8,128)S(1)}, f32[2,12,192]{2,1,0:T(8,128)S(1)}, u32[]{:S(2)}, u32[]{:S(2)}) collective-permute-start(f32[2,12,192]{2,1,0:T(8,128)S(1)} %copy-done.24), channel_id=1, source_target_pairs={{0,2},{2,4},{4,6},{6,0},{1,3},{3,5},{5,7},{7,1},{8,10},{10,12},{12... | collective-permute-start | bytes 55304 | tf_op jit(solution)/shard_map/ppermute | solution.py:239
  63.9 14.1 %collective-permute-start.12 = (f32[2,12,192]{2,1,0:T(8,128)S(1)}, f32[2,12,192]{2,1,0:T(8,128)S(1)}, u32[]{:S(2)}, u32[]{:S(2)}) collective-permute-start(f32[2,12,192]{2,1,0:T(8,128)S(1)} %copy-done.24), channel_id=1, source_target_pairs={{0,6},{2,0},{4,2},{6,4},{1,7},{3,1},{5,3},{7,5},{8,14},{10,8},{12,... | collective-permute-start | bytes 55304 | tf_op jit(solution)/shard_map/ppermute | solution.py:239
  81.0 5.7 %collective-permute-start.13 = (bf16[2,3,48,128]{3,2,1,0:T(8,128)(2,1)S(1)}, bf16[2,3,48,128]{3,2,1,0:T(8,128)(2,1)S(1)}, u32[]{:S(2)}, u32[]{:S(2)}) collective-permute-start(bf16[2,3,48,128]{3,2,1,0:T(8,128)(2,1)S(1)} %get-tuple-element.39), channel_id=1, source_target_pairs={{0,1},{1,0},{8,9},{9,8},{16,17},{17,16},{24,25},{25,24},{2,3},{3,2... | collective-permute-start | bytes 221192 | tf_op jit(solution)/shard_map/ppermute | solution.py:256
  82.1 6.8 %collective-permute-start.14 = (bf16[2,3,48,128]{3,2,1,0:T(8,128)(2,1)S(1)}, bf16[2,3,48,128]{3,2,1,0:T(8,128)(2,1)S(1)}, u32[]{:S(2)}, u32[]{:S(2)}) collective-permute-start(bf16[2,3,48,128]{3,2,1,0:T(8,128)(2,1)S(1)} %get-tuple-element.40), channel_id=1, source_target_pairs={{0,8},{1,9},{8,0},{9,1},{16,24},{17,25},{24,16},{25,17},{2,10},{3,... | collective-permute-start | bytes 221192 | tf_op jit(solution)/shard_map/ppermute | solution.py:256
  84.2 5.7 %collective-permute-start.15 = (bf16[2,3,48,128]{3,2,1,0:T(8,128)(2,1)S(1)}, bf16[2,3,48,128]{3,2,1,0:T(8,128)(2,1)S(1)}, u32[]{:S(2)}, u32[]{:S(2)}) collective-permute-start(bf16[2,3,48,128]{3,2,1,0:T(8,128)(2,1)S(1)} %get-tuple-element.41), channel_id=1, source_target_pairs={{0,9},{1,8},{8,1},{9,0},{16,25},{17,24},{24,17},{25,16},{2,11},{3,... | collective-permute-start | bytes 221192 | tf_op jit(solution)/shard_map/ppermute | solution.py:256
  84.2 5.7 %collective-permute-start.16 = (bf16[2,3,48,128]{3,2,1,0:T(8,128)(2,1)S(1)}, bf16[2,3,48,128]{3,2,1,0:T(8,128)(2,1)S(1)}, u32[]{:S(2)}, u32[]{:S(2)}) collective-permute-start(bf16[2,3,48,128]{3,2,1,0:T(8,128)(2,1)S(1)} %get-tuple-element.42), channel_id=1, source_target_pairs={{0,16},{1,17},{8,24},{9,25},{16,0},{17,1},{24,8},{25,9},{2,18},{3,... | collective-permute-start | bytes 221192 | tf_op jit(solution)/shard_map/ppermute | solution.py:256
  85.6 4.3 %collective-permute-start.17 = (bf16[2,3,48,128]{3,2,1,0:T(8,128)(2,1)S(1)}, bf16[2,3,48,128]{3,2,1,0:T(8,128)(2,1)S(1)}, u32[]{:S(2)}, u32[]{:S(2)}) collective-permute-start(bf16[2,3,48,128]{3,2,1,0:T(8,128)(2,1)S(1)} %get-tuple-element.43), channel_id=1, source_target_pairs={{0,17},{1,16},{8,25},{9,24},{16,1},{17,0},{24,9},{25,8},{2,19},{3,... | collective-permute-start | bytes 221192 | tf_op jit(solution)/shard_map/ppermute | solution.py:256
  86.8 7.6 %collective-permute-start.18 = (bf16[2,3,48,128]{3,2,1,0:T(8,128)(2,1)S(1)}, bf16[2,3,48,128]{3,2,1,0:T(8,128)(2,1)S(1)}, u32[]{:S(2)}, u32[]{:S(2)}) collective-permute-start(bf16[2,3,48,128]{3,2,1,0:T(8,128)(2,1)S(1)} %get-tuple-element.44), channel_id=1, source_target_pairs={{0,24},{1,25},{8,16},{9,17},{16,8},{17,9},{24,0},{25,1},{2,26},{3,... | collective-permute-start | bytes 221192 | tf_op jit(solution)/shard_map/ppermute | solution.py:256
  88.9 5.4 %collective-permute-start.19 = (bf16[2,3,48,128]{3,2,1,0:T(8,128)(2,1)S(1)}, bf16[2,3,48,128]{3,2,1,0:T(8,128)(2,1)S(1)}, u32[]{:S(2)}, u32[]{:S(2)}) collective-permute-start(bf16[2,3,48,128]{3,2,1,0:T(8,128)(2,1)S(1)} %get-tuple-element.45), channel_id=1, source_target_pairs={{0,25},{1,24},{8,17},{9,16},{16,9},{17,8},{24,1},{25,0},{2,27},{3,... | collective-permute-start | bytes 221192 | tf_op jit(solution)/shard_map/ppermute | solution.py:256
  (26 other events, 96.6 us)
where the time goes:
time: 98.6 us; the launch traced here: 97.4 us
  starting transfers between devices  34.9 us (35%)
  waiting for transfers between devices  29.6 us (30%)
  local copies, waits for them, and re-layouts  16.4 us (17%)
  Pallas kernels  12.7 us (13%)
  other arithmetic  2.92 us (3%)
    ppermute x14, starting transfers between devices, swapped(): out[o] = lax.ppermute(blocks[o], GROUP, [(i, i ^ o) for i in range(CHUNKS)])  16.4 us
    unnamed x58, local copies, waits for them, and re-layouts  13.9 us
    ppermute x4, waiting for transfers between devices, shift(): return lax.ppermute(value, axis, pairs)  10.8 us
    ppermute x14, waiting for transfers between devices, swapped(): out[o] = lax.ppermute(blocks[o], GROUP, [(i, i ^ o) for i in range(CHUNKS)])  9.95 us
    all_to_all x2, starting transfers between devices, exchange(): return lax.all_to_all(value, GROUP, 0, 0, tiled=True)  8.95 us
    ppermute x2, waiting for transfers between devices, crossed(): return lax.ppermute(value, ('lon_out', 'lon_in'), pairs)  8.79 us
    pallas_call x1, Pallas kernels, on_device(): pl.pallas_call(functools.partial(main_kernel, rows, band_rows), out_shape...  8.46 us
    ppermute x4, starting transfers between devices, shift(): return lax.ppermute(value, axis, pairs)  4.8 us
  transfers between devices with their start and end apart: 22, of which 5 were waited for; matrix products, arithmetic and copies ran while one was open for 4% of the time, Pallas kernels for 4%

commit v1 on v0

--- a/solution.py
+++ b/solution.py
@@ -18,7 +18,9 @@
 CHUNKS = HEADS * HEAD // LANES
 ROUTES = (5, 7, 4, 6, 1, 3, 2)
 FAR = -1e30
-FLIGHT = 3
+GROUPED = 2
+MAIN_BANDS = 4
+RIM_BANDS = 4
 GROUP = ("lat_in", "lon_in")
 
 
@@ -29,24 +31,29 @@
     return lax.dot_general(a, b, (((da,), (db,)), ((), ())), preferred_element_type=f32)
 
 
-def pack_kernel(me_ref, first_ref, second_ref, *out_refs):
+def pack_kernel(me_ref, held, *out_refs):
     me = me_ref[0]
     for o, out_ref in enumerate(out_refs):
         lanes = pl.ds(pl.multiple_of((me ^ o) * LANES, LANES), LANES)
-        for kv, ref in enumerate((first_ref, second_ref)):
-            for i in range(ref.shape[0]):
+        for kv in range(2):
+            for i in range(held.shape[1]):
                 out_ref[kv, i, 32:] = jnp.zeros((SLOT - 32, LANES), bf16)
-                out_ref[kv, i, :TILE] = ref[i, :, lanes]
+                out_ref[kv, i, :TILE] = held[kv, i, :, lanes]
 
 
 def unpack_kernel(me_ref, *refs):
     me = me_ref[0]
-    outs = refs[CHUNKS:]
-    for o, block_ref in enumerate(refs[:CHUNKS]):
-        lanes = pl.ds(pl.multiple_of((me ^ o) * LANES, LANES), LANES)
-        for kv, ref in enumerate(outs):
-            for i in range(ref.shape[0]):
-                ref[i, :, lanes] = block_ref[kv, i, :TILE]
+    held, sems = refs[CHUNKS + 2 :]
+    copies = []
+    for kv, out in enumerate(refs[CHUNKS : CHUNKS + 2]):
+        for i in range(held.shape[1]):
+            for o, block_ref in enumerate(refs[:CHUNKS]):
+                lanes = pl.ds(pl.multiple_of((me ^ o) * LANES, LANES), LANES)
+                held[kv, i, :, lanes] = block_ref[kv, i, :TILE]
+            copies.append(pltpu.make_async_copy(held.at[kv, i], out.at[i], sems.at[kv, i]))
+            copies[-1].start()
+    for copy in copies:
+        copy.wait()
 
 
 def head_masks():
@@ -77,11 +84,9 @@
     return jnp.concatenate(parts, 0)
 
 
-def interleaved(line, rows):
-    flight = FLIGHT if rows % FLIGHT == 0 else 1
-
+def interleaved(line, rows, flight):
     def step(i, carry):
-        waiting = [line(i * flight + k) for k in range(flight)]
+        waiting = [line(i * flight + k, k) for k in range(flight)]
         live = []
         while waiting or live:
             if waiting:
@@ -92,24 +97,23 @@
     lax.fori_loop(0, rows // flight, step, 0)
 
 
-def main_kernel(rows, band_rows, me_ref, bias_ref, qg_ref, odd_ref, even_ref, cap_ref, *refs):
-    block_refs = refs[:CHUNKS]
-    out_ref, acc, ext, stat_ref = refs[CHUNKS:]
+def main_kernel(rows, band_rows, me_ref, bias_ref, qg_ref, own_odd, own_even, odd_ref, even_ref,
+                cap_ref, out_hbm, acc, stat_ref, ext, out_ref, sems):
     me = me_ref[0]
     side = me & 1
 
-    def place(tile_row, tile, value):
-        for kv in range(2):
-            ext[kv, tile_row + 1, tile] = value[kv]
-
-    for o, ref in enumerate(block_refs):
-        source = me ^ o
+    def place(ref, j, o, tile):
         for i in range(band_rows):
-            place((source >> 1) * band_rows + i, 1 + (source & 1), ref[:, i])
+            row = ((me ^ o) >> 1) * band_rows + i + 1
+            for kv in range(2):
+                ext[kv, row, tile] = ref[j, kv, i]
+
     for j in range(CHUNKS // 2):
-        for ref, o, tile in ((odd_ref, 2 * j + 1, 3 * side), (even_ref, 2 * j, 3 - 3 * side)):
-            for i in range(band_rows):
-                place(((me ^ o) >> 1) * band_rows + i, tile, ref[j, :, i])
+        odd, even = 2 * j + 1, 2 * j
+        place(own_odd, j, odd, 2 - side)
+        place(own_even, j, even, 1 + side)
+        place(odd_ref, j, odd, 3 * side)
+        place(even_ref, j, even, 3 - 3 * side)
     for end in range(2):
         for kv in range(2):
             ext[kv, end * (rows + 1)] = cap_ref[end, kv]
@@ -132,18 +136,17 @@
         rim = jnp.concatenate(
             [jnp.concatenate([ext[kv, r + a, 0], ext[kv, r + a, 3]], 1) for a in range(3)], 0
         )
-        return inside, rim, jnp.concatenate([jnp.concatenate([inside, inside], 1), rim], 0)
-
-    def line(r):
+        return jnp.concatenate([jnp.concatenate([inside, inside], 1), rim], 0)
+
+    def line(r, k):
         band, inner = r // band_rows, r % band_rows
         scale = jnp.asarray(HEAD**-0.5, bf16)
         q_two, q_split = stacked([qg_ref[band * 2 + x, 0, inner] * scale for x in range(2)], masks)
         g_two, g_split = stacked([qg_ref[band * 2 + x, 1, inner] for x in range(2)], masks)
-        k_in, k_rim, k_all = gathered(0, r)
-        v_in, v_rim, v_all = gathered(1, r)
-        yield
-        scores = jnp.concatenate([dot(k_in, q_two, 1, 1), dot(k_rim, q_split, 1, 1)], 0)
-        grad_probs = jnp.concatenate([dot(v_in, g_two, 1, 1), dot(v_rim, g_split, 1, 1)], 0)
+        k_all, v_all = gathered(0, r), gathered(1, r)
+        yield
+        scores = dot(k_all, q_split, 1, 1)
+        grad_probs = dot(v_all, g_split, 1, 1)
         yield
         shifted = biased(scores, [bias_ref[r, j : j + 1] for j in range(NPAIR)], pad)
         top = jnp.max(shifted, axis=0, keepdims=True)
@@ -170,42 +173,77 @@
         dq = merge(dot(slopes, k_all, 0, 0) * HEAD**-0.5)
         for x in range(2):
             out_ref[band * 2 + x, 1, inner] = dq[x].astype(bf16)
-        yield
         for kv, left, two in ((0, slopes, q_two), (1, probs, g_two)):
             inside = dot(left[: 6 * SLOT], two, 1, 0)
             for a in range(3):
                 for x in range(2):
                     at = (2 * a + x) * SLOT
                     acc[kv, r + a, x] += inside[at : at + SLOT]
-
-    interleaved(line, rows)
-
-
-def rim_kernel(rows, band_rows, me_ref, bias_ref, ext, sum_ref, west_ref, east_ref,
-               west_stat, east_stat, *refs):
+        if k % band_rows == band_rows - 1:
+            send(band).start()
+
+    def send(group):
+        part = pl.ds(group * GROUPED, GROUPED)
+        return pltpu.make_async_copy(
+            out_ref.at[part], out_hbm.at[part], sems.at[group]
+        )
+
+    flight = MAIN_BANDS * band_rows if rows % (MAIN_BANDS * band_rows) == 0 else band_rows
+
+    interleaved(line, rows, flight)
+    for band in range(rows // band_rows):
+        send(band).wait()
+
+
+def rim_kernel(rows, band_rows, capped, me_ref, bias_ref, own_even, own_odd, edge_ref, sum_ref,
+               east_hbm, west_hbm, stat_ref, *refs):
     block_refs = refs[:CHUNKS]
-    cap_ref, acc = refs[CHUNKS:]
+    acc, ext, guest_ref, sems = refs[-4:]
     me = me_ref[0]
+    bands = rows // band_rows
+
+    def guest(e, band):
+        ref = (east_hbm, west_hbm)[e]
+        at = sems.at[e * bands + band]
+        return pltpu.make_async_copy(ref.at[band], guest_ref.at[e, band], at)
+
+    for band in range(min(2, bands)):
+        for e in range(2):
+            guest(e, band).start()
+    for o in range(CHUNKS):
+        for i in range(band_rows):
+            row = ((me ^ o) >> 1) * band_rows + i + 1
+            for kv in range(2):
+                ext[kv, row, (me ^ o) & 1] = (own_even, own_odd)[o & 1][o >> 1, kv, i]
+    for kv in range(2):
+        for end in range(2):
+            for x in range(2):
+                ext[kv, end * (rows + 1), x] = edge_ref[end, kv, x]
     masks = head_masks()
     pad = pad_rows()
-    from_east = lax.broadcasted_iota(jnp.int32, (1, WIDTH), 1) < HALF
     acc[...] = sum_ref[...]
 
-    def line(r):
+    def line(r, k):
         band, inner = r // band_rows, r % band_rows
+        if k % band_rows == 0:
+            for e in range(2):
+                guest(e, band).wait()
+
+            @pl.when(band + 2 < bands)
+            def _():
+                for e in range(2):
+                    guest(e, jnp.minimum(band + 2, bands - 1)).start()
+
         scale = jnp.asarray(HEAD**-0.5, bf16)
-        q_split = stacked([ref[band, 0, inner] * scale for ref in (east_ref, west_ref)], masks)[1]
-        g_split = stacked([ref[band, 1, inner] for ref in (east_ref, west_ref)], masks)[1]
+        q_split = stacked([guest_ref[e, band, 0, inner] * scale for e in range(2)], masks)[1]
+        g_split = stacked([guest_ref[e, band, 1, inner] for e in range(2)], masks)[1]
         k_own, v_own = [
             jnp.concatenate(
-                [jnp.concatenate([ext[kv, r + a, 2], ext[kv, r + a, 1]], 1) for a in range(3)], 0
+                [jnp.concatenate([ext[kv, r + a, x] for x in (1, 0)], 1) for a in range(3)], 0
             )
             for kv in range(2)
         ]
-        lse, delta = [
-            jnp.where(from_east, east_stat[s, pl.ds(r, 1)], west_stat[s, pl.ds(r, 1)])
-            for s in range(2)
-        ]
+        lse, delta = [stat_ref[s, pl.ds(r, 1)] for s in range(2)]
         yield
         scores = dot(k_own, q_split, 1, 1)
         grad_probs = dot(v_own, g_split, 1, 1)
@@ -221,16 +259,19 @@
                 acc[kv, r + a, 1] += part[a * SLOT : (a + 1) * SLOT, :LANES]
                 acc[kv, r + a, 0] += part[a * SLOT : (a + 1) * SLOT, LANES:]
 
-    interleaved(line, rows)
+    flight = RIM_BANDS * band_rows if rows % (RIM_BANDS * band_rows) == 0 else band_rows
+
+    interleaved(line, rows, flight)
     for o, ref in enumerate(block_refs):
         target = me ^ o
         for kv in range(2):
             for i in range(band_rows):
                 row = (target >> 1) * band_rows + i + 1
                 ref[kv, i] = acc[kv, row, target & 1].astype(bf16)
-    for end in range(2):
-        for kv in range(2):
-            cap_ref[end, kv] = acc[kv, end * (rows + 1)].astype(bf16)
+    if capped:
+        for end in range(2):
+            for kv in range(2):
+                refs[CHUNKS][end, kv] = acc[kv, end * (rows + 1)].astype(bf16)
 
 
 def shift(value, axis, by, wrap):
@@ -300,7 +341,8 @@
     me_list = me.reshape(1)
     smem = pl.BlockSpec(memory_space=pltpu.SMEM)
     vmem = pl.BlockSpec(memory_space=pltpu.VMEM)
-    params = pltpu.CompilerParams(vmem_limit_bytes=32 * 2**20)
+    anywhere = pl.BlockSpec(memory_space=pl.ANY)
+    params = pltpu.CompilerParams(vmem_limit_bytes=16 * 2**20)
     block = jax.ShapeDtypeStruct((2, band_rows, SLOT, LANES), bf16)
     natural = jnp.arange(CHUNKS, dtype=jnp.int32) ^ me
 
@@ -313,14 +355,14 @@
     blocks = pl.pallas_call(
         pack_kernel,
         out_shape=(block,) * CHUNKS,
-        in_specs=[smem, vmem, vmem],
+        in_specs=[smem, vmem],
         out_specs=(vmem,) * CHUNKS,
         compiler_params=params,
         name="pack_keys",
-    )(me_list, keys, values)
+    )(me_list, jnp.stack([keys, values]))
     blocks = swapped(blocks)
-    odd = crossed(jnp.stack(blocks[1::2]), 1)
-    even = crossed(jnp.stack(blocks[0::2]), -1)
+    own_odd, own_even = jnp.stack(blocks[1::2]), jnp.stack(blocks[0::2])
+    odd, even = crossed(own_odd, 1), crossed(own_even, -1)
     qg = exchange(packed(queries, cotangent))
     west = shift(halves(qg)[:, 1], "lon_out", 1, True)
     east = shift(halves(qg)[:, 0], "lon_out", -1, True)
@@ -344,34 +386,45 @@
         caps = jnp.zeros((2, 2, 4, SLOT, LANES), bf16)
         first_row = 0
     bias = bias_table(pair_list, quad_index, quad_table, first_row, rows)
-    out, acc, ext, stats = pl.pallas_call(
+    out, acc, stats = pl.pallas_call(
         functools.partial(main_kernel, rows, band_rows),
         out_shape=(
             jax.ShapeDtypeStruct(qg.shape, bf16),
-            jax.ShapeDtypeStruct((2, rows + 2, 2, SLOT, LANES), f32),
-            jax.ShapeDtypeStruct((2, rows + 2, 4, SLOT, LANES), bf16),
+            jax.ShapeDtypeStruct((2, rows + 3, 2, SLOT, LANES), f32),
             jax.ShapeDtypeStruct((2, rows, WIDTH), f32),
         ),
-        in_specs=[smem] + [vmem] * (5 + CHUNKS),
-        out_specs=(vmem,) * 4,
+        in_specs=[smem] + [vmem] * 7,
+        out_specs=(anywhere, vmem, vmem),
+        scratch_shapes=[
+            pltpu.VMEM((2, rows + 2, 4, SLOT, LANES), bf16),
+            pltpu.VMEM(qg.shape, bf16),
+            pltpu.SemaphoreType.DMA((bands,)),
+        ],
         compiler_params=params,
         name="main_rows",
-    )(me_list, bias, qg, odd, even, caps, *blocks)
-    west_stat = shift(stats, "lon_out", 1, True)
-    east_stat = shift(stats, "lon_out", -1, True)
+    )(me_list, bias, qg, own_odd, own_even, odd, even, caps)
+    from_west = shift(stats, "lon_out", 1, True)
+    from_east = shift(stats, "lon_out", -1, True)
+    lane = jnp.arange(WIDTH, dtype=jnp.int32)
+    stats = jnp.where(lane < HALF, from_east, from_west)
     out = exchange(out)
+    cap_shape = (jax.ShapeDtypeStruct((2, 2, 2, SLOT, LANES), bf16),)
+    cap_shape = cap_shape if lat_groups > 1 else ()
     grads = pl.pallas_call(
-        functools.partial(rim_kernel, rows, band_rows),
-        out_shape=(block,) * CHUNKS
-        + (jax.ShapeDtypeStruct((2, 2, 2, SLOT, LANES), bf16),),
-        in_specs=[smem] + [vmem] * 7,
-        out_specs=(vmem,) * (CHUNKS + 1),
-        scratch_shapes=[pltpu.VMEM(acc.shape, f32)],
+        functools.partial(rim_kernel, rows, band_rows, lat_groups > 1),
+        out_shape=(block,) * CHUNKS + cap_shape,
+        in_specs=[smem] + [vmem] * 5 + [anywhere] * 2 + [vmem],
+        out_specs=(vmem,) * (CHUNKS + len(cap_shape)),
+        scratch_shapes=[
+            pltpu.VMEM((2, rows + 2, 2, SLOT, LANES), t) for t in (f32, bf16)
+        ]
+        + [pltpu.VMEM((2,) + west.shape, bf16), pltpu.SemaphoreType.DMA((2 * bands,))],
         compiler_params=params,
         name="rim_rows",
-    )(me_list, bias, ext, acc, west, east, west_stat, east_stat)
-    blocks, cap = grads[:CHUNKS], grads[CHUNKS]
+    )(me_list, bias, own_even, own_odd, caps[:, :, 1:3], acc[:, : rows + 2], east, west, stats)
+    blocks = grads[:CHUNKS]
     if lat_groups > 1:
+        cap = grads[CHUNKS]
         north = shift(cap[1], "lat_out", 1, False).astype(f32)
         south = shift(cap[0], "lat_out", -1, False).astype(f32)
         whole = halves(jnp.stack(blocks)[natural]).astype(f32)
@@ -385,7 +438,11 @@
         unpack_kernel,
         out_shape=(tile, tile),
         in_specs=[smem] + [vmem] * CHUNKS,
-        out_specs=(vmem, vmem),
+        out_specs=(anywhere, anywhere),
+        scratch_shapes=[
+            pltpu.VMEM((2,) + queries.shape, bf16),
+            pltpu.SemaphoreType.DMA((2, band_rows)),
+        ],
         compiler_params=params,
         name="unpack_grads",
     )(me_list, *blocks)

time: 98.6 us -> 82.9 us (0.84)
  local copies, waits for them, and re-layouts: 16.4 us -> 1.65 us
  waiting for transfers between devices: 29.6 us -> 32.5 us
  Pallas kernels: 12.7 us -> 10.6 us
  starting transfers between devices: 34.9 us -> 33.7 us
    unnamed x58 -> x12, local copies, waits for them, and re-layouts: 13.9 us -> 0.12 us
    ppermute x4, waiting for transfers between devices: 10.8 us -> 12.9 us  [shift(): return lax.ppermute(value, axis, pairs)]
    pallas_call x1, Pallas kernels: 8.46 us -> 6.43 us  [on_device(): pl.pallas_call(functools.partial(main_kernel, rows, band_rows), out_shape...]
    another operation x2 -> x3, other arithmetic: 0.08 us -> 1.24 us  [the longest x1 1.17 us: on_device(): jnp.stack([keys, values])]
    transpose x1, other arithmetic: 2.04 us -> 0.95 us  [packed(): return split.transpose(3, 0, 1, 2, 4)]
    reshape x1, local copies, waits for them, and re-layouts: 1.13 us -> 0.06 us  [unpacked(): joined = moved.reshape(moved.shape[:3] + (moved.shape[3] * LANES,))]
  transfers between devices with their start and end apart: 22 -> 22, of which waited for: 5 -> 6; matrix products, arithmetic and copies ran while one was open for 4% -> 3% of each run, Pallas kernels for 4% -> 5%
where the time goes in v1:
time: 82.9 us; the launch traced here: 82.2 us
  starting transfers between devices  33.7 us (41%)
  waiting for transfers between devices  32.5 us (39%)
  Pallas kernels  10.6 us (13%)
  other arithmetic  3 us (4%)
  local copies, waits for them, and re-layouts  1.65 us (2%)
  between operations  0.86 us (1%)
    ppermute x14, starting transfers between devices, swapped(): out[o] = lax.ppermute(blocks[o], GROUP, [(i, i ^ o) for i in range(CHUNKS)])  16.1 us
    ppermute x4, waiting for transfers between devices, shift(): return lax.ppermute(value, axis, pairs)  12.9 us
    ppermute x14, waiting for transfers between devices, swapped(): out[o] = lax.ppermute(blocks[o], GROUP, [(i, i ^ o) for i in range(CHUNKS)])  10 us
    ppermute x2, waiting for transfers between devices, crossed(): return lax.ppermute(value, ('lon_out', 'lon_in'), pairs)  9.54 us
    all_to_all x2, starting transfers between devices, exchange(): return lax.all_to_all(value, GROUP, 0, 0, tiled=True)  8.13 us
    pallas_call x1, Pallas kernels, on_device(): pl.pallas_call(functools.partial(main_kernel, rows, band_rows), out_shape...  6.43 us
    ppermute x4, starting transfers between devices, shift(): return lax.ppermute(value, axis, pairs)  4.77 us
    ppermute x2, starting transfers between devices, crossed(): return lax.ppermute(value, ('lon_out', 'lon_in'), pairs)  4.72 us
  transfers between devices with their start and end apart: 22, of which 6 were waited for; matrix products, arithmetic and copies ran while one was open for 3% of the time, Pallas kernels for 5%

profile of v1, /device:TPU:1, one launch (start us, length us, event | category | flops | bytes accessed | tf_op | source)
XLA Modules:
  0.0 82.2 jit_solution(11433285223779852464)
XLA Ops:
  0.7 1.2 %pad_maximum_fusion.held = bf16[2,3,45,1024]{3,2,1,0:T(8,128)(2,1)S(1)} fusion(bf16[1,3,45,1024]{3,2,1,0:T(8,128)(2,1)} %bitcast.51, bf16[1,3,45,1024]{3,2,1,0:T(8,128)(2,1)} %bitcast.52), kind=kLoop, calls=%fused_computation.7 | loop fusion | flops 276480 | bytes 1105920 | tf_op jit(solution)/shard_map/stack | solution.py:362
  2.1 2.7 %collective-permute-start.5 = (bf16[2,3,48,128]{3,2,1,0:T(8,128)(2,1)S(1)}, bf16[2,3,48,128]{3,2,1,0:T(8,128)(2,1)S(1)}, u32[]{:S(2)}, u32[]{:S(2)}) collective-permute-start(bf16[2,3,48,128]{3,2,1,0:T(8,128)(2,1)S(1)} %get-tuple-element.31), channel_id=1, source_target_pairs={{0,16},{1,17},{8,24},{9,25},{16,0},{17,1},{24,8},{25,9},{2,18},{3,... | collective-permute-start | bytes 221192 | tf_op jit(solution)/shard_map/ppermute | solution.py:297
  4.8 1.6 %collective-permute-start = (bf16[2,3,48,128]{3,2,1,0:T(8,128)(2,1)S(1)}, bf16[2,3,48,128]{3,2,1,0:T(8,128)(2,1)S(1)}, u32[]{:S(2)}, u32[]{:S(2)}) collective-permute-start(bf16[2,3,48,128]{3,2,1,0:T(8,128)(2,1)S(1)} %get-tuple-element.25), channel_id=1, source_target_pairs={{0,1},{1,0},{8,9},{9,8},{16,17},{17,16},{24,25},{25,24},{2,3},{3,2... | collective-permute-start | bytes 221192 | tf_op jit(solution)/shard_map/ppermute | solution.py:297
  7.8 4.1 %all-to-all-start = ((bf16[8,2,3,48,128]{4,3,2,1,0:T(8,128)(2,1)}), bf16[8,2,3,48,128]{4,3,2,1,0:T(8,128)(2,1)S(1)}, u32[]{:S(2)}, u32[]{:S(2)}) async-start(bf16[8,2,3,48,128]{4,3,2,1,0:T(8,128)(2,1)} %bitcast_bitcast_fusion), calls=%async_computation | async-start | bytes 1179648 | tf_op jit(solution)/shard_map/all_to_all | solution.py:350
  13.1 2.3 %collective-permute-start.2 = (bf16[2,3,48,128]{3,2,1,0:T(8,128)(2,1)S(1)}, bf16[2,3,48,128]{3,2,1,0:T(8,128)(2,1)S(1)}, u32[]{:S(2)}, u32[]{:S(2)}) collective-permute-start(bf16[2,3,48,128]{3,2,1,0:T(8,128)(2,1)S(1)} %get-tuple-element.27), channel_id=1, source_target_pairs={{0,17},{1,16},{8,25},{9,24},{16,1},{17,0},{24,9},{25,8},{2,19},{3,... | collective-permute-start | bytes 221192 | tf_op jit(solution)/shard_map/ppermute | solution.py:297
  15.8 3.4 %collective-permute-start.8 = (bf16[4,2,3,48,128]{4,3,2,1,0:T(8,128)(2,1)S(1)}, bf16[4,2,3,48,128]{4,3,2,1,0:T(8,128)(2,1)S(1)}, u32[]{:S(2)}, u32[]{:S(2)}) collective-permute-start(bf16[4,2,3,48,128]{4,3,2,1,0:T(8,128)(2,1)S(1)} %pad_maximum_fusion.2.own_even), channel_id=1, source_target_pairs={{0,6},{1,3},{2,0},{3,5},{4,2},{5,7},{6,4},{7,1},{8,14},{9,11},{10,... | collective-permute-start | bytes 884744 | tf_op jit(solution)/shard_map/ppermute | solution.py:290
  19.2 3.7 %collective-permute-done.2 = bf16[2,3,48,128]{3,2,1,0:T(8,128)(2,1)S(1)} collective-permute-done((bf16[2,3,48,128]{3,2,1,0:T(8,128)(2,1)S(1)}, bf16[2,3,48,128]{3,2,1,0:T(8,128)(2,1)S(1)}, u32[]{:S(2)}, u32[]{:S(2)}) %collective-permute-start.2) | collective-permute-done | bytes 73760 | tf_op jit(solution)/shard_map/ppermute | solution.py:297
  22.9 1.9 %collective-permute-done.3 = bf16[2,3,48,128]{3,2,1,0:T(8,128)(2,1)S(1)} collective-permute-done((bf16[2,3,48,128]{3,2,1,0:T(8,128)(2,1)S(1)}, bf16[2,3,48,128]{3,2,1,0:T(8,128)(2,1)S(1)}, u32[]{:S(2)}, u32[]{:S(2)}) %collective-permute-start.3) | collective-permute-done | bytes 73760 | tf_op jit(solution)/shard_map/ppermute | solution.py:297
  24.8 1.3 %collective-permute-start.7 = (bf16[4,2,3,48,128]{4,3,2,1,0:T(8,128)(2,1)S(1)}, bf16[4,2,3,48,128]{4,3,2,1,0:T(8,128)(2,1)S(1)}, u32[]{:S(2)}, u32[]{:S(2)}) collective-permute-start(bf16[4,2,3,48,128]{4,3,2,1,0:T(8,128)(2,1)S(1)} %pad_maximum_fusion.1.own_odd), channel_id=1, source_target_pairs={{0,2},{1,7},{2,4},{3,1},{4,6},{5,3},{6,0},{7,5},{8,10},{9,15},{10,... | collective-permute-start | bytes 884744 | tf_op jit(solution)/shard_map/ppermute | solution.py:290
  26.3 9.5 %collective-permute-done.7.odd_ref = bf16[4,2,3,48,128]{4,3,2,1,0:T(8,128)(2,1)S(1)} collective-permute-done((bf16[4,2,3,48,128]{4,3,2,1,0:T(8,128)(2,1)S(1)}, bf16[4,2,3,48,128]{4,3,2,1,0:T(8,128)(2,1)S(1)}, u32[]{:S(2)}, u32[]{:S(2)}) %collective-permute-start.7) | collective-permute-done | bytes 294944 | tf_op jit(solution)/shard_map/ppermute | solution.py:290
  35.8 6.4 %main_rows.1 = (bf16[8,2,3,48,128]{4,3,2,1,0:T(8,128)(2,1)}, f32[2,15,2,48,128]{4,3,2,1,0:T(8,128)S(1)}, f32[2,12,192]{2,1,0:T(8,128)S(1)}) custom-call(s32[1]{0:T(128)} %bitcast.me_ref, f32[12,9,192]{2,1,0:T(8,128)S(1)} %broadcast_select_fusion.bias_ref, bf16[8,2,3,48,128]{4,3,2,1,0:T(8,128)(2,1)S(1)} %all-to-all-done.qg_ref, ...), custom_call_target="tpu_custom_call" | custom-call | tf_op jit(solution)/shard_map/main_rows/pallas_call | solution.py:389
  42.3 4.1 %all-to-all-start.1 = ((bf16[8,2,3,48,128]{4,3,2,1,0:T(8,128)(2,1)}), bf16[8,2,3,48,128]{4,3,2,1,0:T(8,128)(2,1)S(1)}, u32[]{:S(2)}, u32[]{:S(2)}) async-start(bf16[8,2,3,48,128]{4,3,2,1,0:T(8,128)(2,1)} %get-tuple-element.33), calls=%async_computation.1 | async-start | bytes 1179648 | tf_op jit(solution)/shard_map/all_to_all | solution.py:350
  46.5 3.3 %collective-permute-start.9 = (bf16[4,2,3,48,128]{4,3,2,1,0:T(8,128)(2,1)S(1)}, bf16[4,2,3,48,128]{4,3,2,1,0:T(8,128)(2,1)S(1)}, u32[]{:S(2)}, u32[]{:S(2)}) collective-permute-start(bf16[4,2,3,48,128]{4,3,2,1,0:T(8,128)(2,1)S(1)} %get-tuple-element.47), channel_id=1, source_target_pairs={{0,6},{2,0},{4,2},{6,4},{1,7},{3,1},{5,3},{7,5},{8,14},{10,8},{12,... | collective-permute-start | bytes 884744 | tf_op jit(solution)/shard_map/ppermute | solution.py:280
  49.7 1.4 %collective-permute-start.12 = (f32[2,12,192]{2,1,0:T(8,128)S(1)}, f32[2,12,192]{2,1,0:T(8,128)S(1)}, u32[]{:S(2)}, u32[]{:S(2)}) collective-permute-start(f32[2,12,192]{2,1,0:T(8,128)S(1)} %get-tuple-element.35), channel_id=1, source_target_pairs={{0,2},{2,4},{4,6},{6,0},{1,3},{3,5},{5,7},{7,1},{8,10},{10,12},{12... | collective-permute-start | bytes 55304 | tf_op jit(solution)/shard_map/ppermute | solution.py:280
  51.3 10.7 %collective-permute-done.11 = f32[2,12,192]{2,1,0:T(8,128)S(1)} collective-permute-done((f32[2,12,192]{2,1,0:T(8,128)S(1)}, f32[2,12,192]{2,1,0:T(8,128)S(1)}, u32[]{:S(2)}, u32[]{:S(2)}) %collective-permute-start.11) | collective-permute-done | bytes 18464 | tf_op jit(solution)/shard_map/ppermute | solution.py:280
  62.0 2.2 %collective-permute-done.12 = f32[2,12,192]{2,1,0:T(8,128)S(1)} collective-permute-done((f32[2,12,192]{2,1,0:T(8,128)S(1)}, f32[2,12,192]{2,1,0:T(8,128)S(1)}, u32[]{:S(2)}, u32[]{:S(2)}) %collective-permute-start.12) | collective-permute-done | bytes 18464 | tf_op jit(solution)/shard_map/ppermute | solution.py:280
  64.2 3.1 %rim_rows.1 = (bf16[2,3,48,128]{3,2,1,0:T(8,128)(2,1)S(1)}, bf16[2,3,48,128]{3,2,1,0:T(8,128)(2,1)S(1)}, bf16[2,3,48,128]{3,2,1,0:T(8,128)(2,1)S(1)}, bf16[2,3,4...) custom-call(s32[1]{0:T(128)} %bitcast.me_ref, ...), custom_call_target="tpu_custom_call" | custom-call | tf_op jit(solution)/shard_map/rim_rows/pallas_call | solution.py:413
  67.3 1.1 %collective-permute-start.13 = (bf16[2,3,48,128]{3,2,1,0:T(8,128)(2,1)S(1)}, bf16[2,3,48,128]{3,2,1,0:T(8,128)(2,1)S(1)}, u32[]{:S(2)}, u32[]{:S(2)}) collective-permute-start(bf16[2,3,48,128]{3,2,1,0:T(8,128)(2,1)S(1)} %get-tuple-element.37), channel_id=1, source_target_pairs={{0,1},{1,0},{8,9},{9,8},{16,17},{17,16},{24,25},{25,24},{2,3},{3,2... | collective-permute-start | bytes 221192 | tf_op jit(solution)/shard_map/ppermute | solution.py:297
  68.5 1.8 %collective-permute-start.14 = (bf16[2,3,48,128]{3,2,1,0:T(8,128)(2,1)S(1)}, bf16[2,3,48,128]{3,2,1,0:T(8,128)(2,1)S(1)}, u32[]{:S(2)}, u32[]{:S(2)}) collective-permute-start(bf16[2,3,48,128]{3,2,1,0:T(8,128)(2,1)S(1)} %get-tuple-element.38), channel_id=1, source_target_pairs={{0,8},{1,9},{8,0},{9,1},{16,24},{17,25},{24,16},{25,17},{2,10},{3,... | collective-permute-start | bytes 221192 | tf_op jit(solution)/shard_map/ppermute | solution.py:297
  70.3 1.4 %collective-permute-start.16 = (bf16[2,3,48,128]{3,2,1,0:T(8,128)(2,1)S(1)}, bf16[2,3,48,128]{3,2,1,0:T(8,128)(2,1)S(1)}, u32[]{:S(2)}, u32[]{:S(2)}) collective-permute-start(bf16[2,3,48,128]{3,2,1,0:T(8,128)(2,1)S(1)} %get-tuple-element.40), channel_id=1, source_target_pairs={{0,16},{1,17},{8,24},{9,25},{16,0},{17,1},{24,8},{25,9},{2,18},{3,... | collective-permute-start | bytes 221192 | tf_op jit(solution)/shard_map/ppermute | solution.py:297
  71.6 1.2 %collective-permute-start.17 = (bf16[2,3,48,128]{3,2,1,0:T(8,128)(2,1)S(1)}, bf16[2,3,48,128]{3,2,1,0:T(8,128)(2,1)S(1)}, u32[]{:S(2)}, u32[]{:S(2)}) collective-permute-start(bf16[2,3,48,128]{3,2,1,0:T(8,128)(2,1)S(1)} %get-tuple-element.41), channel_id=1, source_target_pairs={{0,17},{1,16},{8,25},{9,24},{16,1},{17,0},{24,9},{25,8},{2,19},{3,... | collective-permute-start | bytes 221192 | tf_op jit(solution)/shard_map/ppermute | solution.py:297
  72.8 2.2 %collective-permute-start.18 = (bf16[2,3,48,128]{3,2,1,0:T(8,128)(2,1)S(1)}, bf16[2,3,48,128]{3,2,1,0:T(8,128)(2,1)S(1)}, u32[]{:S(2)}, u32[]{:S(2)}) collective-permute-start(bf16[2,3,48,128]{3,2,1,0:T(8,128)(2,1)S(1)} %get-tuple-element.42), channel_id=1, source_target_pairs={{0,24},{1,25},{8,16},{9,17},{16,8},{17,9},{24,0},{25,1},{2,26},{3,... | collective-permute-start | bytes 221192 | tf_op jit(solution)/shard_map/ppermute | solution.py:297
  75.0 1.0 %collective-permute-start.19 = (bf16[2,3,48,128]{3,2,1,0:T(8,128)(2,1)S(1)}, bf16[2,3,48,128]{3,2,1,0:T(8,128)(2,1)S(1)}, u32[]{:S(2)}, u32[]{:S(2)}) collective-permute-start(bf16[2,3,48,128]{3,2,1,0:T(8,128)(2,1)S(1)} %get-tuple-element.43), channel_id=1, source_target_pairs={{0,25},{1,24},{8,17},{9,16},{16,9},{17,8},{24,1},{25,0},{2,27},{3,... | collective-permute-start | bytes 221192 | tf_op jit(solution)/shard_map/ppermute | solution.py:297
  75.9 4.4 %collective-permute-done.18.refs_6_ = bf16[2,3,48,128]{3,2,1,0:T(8,128)(2,1)S(1)} collective-permute-done((bf16[2,3,48,128]{3,2,1,0:T(8,128)(2,1)S(1)}, bf16[2,3,48,128]{3,2,1,0:T(8,128)(2,1)S(1)}, u32[]{:S(2)}, u32[]{:S(2)}) %collective-permute-start.18) | collective-permute-done | bytes 73760 | tf_op jit(solution)/shard_map/ppermute | solution.py:297
  (66 shorter events, 5.5 us)
Async XLA Ops:
  0.6 6.2 %copy-start.1 = (bf16[3,45,1024]{2,1,0:T(8,128)(2,1)S(1)}, bf16[3,45,1024]{2,1,0:T(8,128)(2,1)}, u32[]{:S(2)}) copy-start(bf16[3,45,1024]{2,1,0:T(8,128)(2,1)} %param.7) | copy-start | bytes 829444
  0.6 6.2 %copy-start = (bf16[3,45,1024]{2,1,0:T(8,128)(2,1)S(1)}, bf16[3,45,1024]{2,1,0:T(8,128)(2,1)}, u32[]{:S(2)}) copy-start(bf16[3,45,1024]{2,1,0:T(8,128)(2,1)} %param.10) | copy-start | bytes 829444
  2.0 11.1 %collective-permute-start.4 = (bf16[2,3,48,128]{3,2,1,0:T(8,128)(2,1)S(1)}, bf16[2,3,48,128]{3,2,1,0:T(8,128)(2,1)S(1)}, u32[]{:S(2)}, u32[]{:S(2)}) collective-permute-start(bf16[2,3,48,128]{3,2,1,0:T(8,128)(2,1)S(1)} %get-tuple-element.30), channel_id=1, source_target_pairs={{0,8},{1,9},{8,0},{9,1},{16,24},{17,25},{24,16},{25,17},{2,10},{3,... | collective-permute-start | bytes 221192 | tf_op jit(solution)/shard_map/ppermute | solution.py:297
  2.1 13.3 %collective-permute-start.5 = (bf16[2,3,48,128]{3,2,1,0:T(8,128)(2,1)S(1)}, bf16[2,3,48,128]{3,2,1,0:T(8,128)(2,1)S(1)}, u32[]{:S(2)}, u32[]{:S(2)}) collective-permute-start(bf16[2,3,48,128]{3,2,1,0:T(8,128)(2,1)S(1)} %get-tuple-element.31), channel_id=1, source_target_pairs={{0,16},{1,17},{8,24},{9,25},{16,0},{17,1},{24,8},{25,9},{2,18},{3,... | collective-permute-start | bytes 221192 | tf_op jit(solution)/shard_map/ppermute | solution.py:297
  4.8 10.9 %collective-permute-start.6 = (bf16[2,3,48,128]{3,2,1,0:T(8,128)(2,1)S(1)}, bf16[2,3,48,128]{3,2,1,0:T(8,128)(2,1)S(1)}, u32[]{:S(2)}, u32[]{:S(2)}) collective-permute-start(bf16[2,3,48,128]{3,2,1,0:T(8,128)(2,1)S(1)} %get-tuple-element.32), channel_id=1, source_target_pairs={{0,24},{1,25},{8,16},{9,17},{16,8},{17,9},{24,0},{25,1},{2,26},{3,... | collective-permute-start | bytes 221192 | tf_op jit(solution)/shard_map/ppermute | solution.py:297
  4.8 14.3 %collective-permute-start = (bf16[2,3,48,128]{3,2,1,0:T(8,128)(2,1)S(1)}, bf16[2,3,48,128]{3,2,1,0:T(8,128)(2,1)S(1)}, u32[]{:S(2)}, u32[]{:S(2)}) collective-permute-start(bf16[2,3,48,128]{3,2,1,0:T(8,128)(2,1)S(1)} %get-tuple-element.25), channel_id=1, source_target_pairs={{0,1},{1,0},{8,9},{9,8},{16,17},{17,16},{24,25},{25,24},{2,3},{3,2... | collective-permute-start | bytes 221192 | tf_op jit(solution)/shard_map/ppermute | solution.py:297
  6.5 12.7 %collective-permute-start.1 = (bf16[2,3,48,128]{3,2,1,0:T(8,128)(2,1)S(1)}, bf16[2,3,48,128]{3,2,1,0:T(8,128)(2,1)S(1)}, u32[]{:S(2)}, u32[]{:S(2)}) collective-permute-start(bf16[2,3,48,128]{3,2,1,0:T(8,128)(2,1)S(1)} %get-tuple-element.26), channel_id=1, source_target_pairs={{0,9},{1,8},{8,1},{9,0},{16,25},{17,24},{24,17},{25,16},{2,11},{3,... | collective-permute-start | bytes 221192 | tf_op jit(solution)/shard_map/ppermute | solution.py:297
  7.8 28.0 %all-to-all-start = ((bf16[8,2,3,48,128]{4,3,2,1,0:T(8,128)(2,1)}), bf16[8,2,3,48,128]{4,3,2,1,0:T(8,128)(2,1)S(1)}, u32[]{:S(2)}, u32[]{:S(2)}) async-start(bf16[8,2,3,48,128]{4,3,2,1,0:T(8,128)(2,1)} %bitcast_bitcast_fusion), calls=%async_computation | async-start | bytes 1179648 | tf_op jit(solution)/shard_map/all_to_all | solution.py:350
  13.1 9.8 %collective-permute-start.2 = (bf16[2,3,48,128]{3,2,1,0:T(8,128)(2,1)S(1)}, bf16[2,3,48,128]{3,2,1,0:T(8,128)(2,1)S(1)}, u32[]{:S(2)}, u32[]{:S(2)}) collective-permute-start(bf16[2,3,48,128]{3,2,1,0:T(8,128)(2,1)S(1)} %get-tuple-element.27), channel_id=1, source_target_pairs={{0,17},{1,16},{8,25},{9,24},{16,1},{17,0},{24,9},{25,8},{2,19},{3,... | collective-permute-start | bytes 221192 | tf_op jit(solution)/shard_map/ppermute | solution.py:297
  15.4 9.4 %collective-permute-start.3 = (bf16[2,3,48,128]{3,2,1,0:T(8,128)(2,1)S(1)}, bf16[2,3,48,128]{3,2,1,0:T(8,128)(2,1)S(1)}, u32[]{:S(2)}, u32[]{:S(2)}) collective-permute-start(bf16[2,3,48,128]{3,2,1,0:T(8,128)(2,1)S(1)} %get-tuple-element.28), channel_id=1, source_target_pairs={{0,25},{1,24},{8,17},{9,16},{16,9},{17,8},{24,1},{25,0},{2,27},{3,... | collective-permute-start | bytes 221192 | tf_op jit(solution)/shard_map/ppermute | solution.py:297
  15.8 10.5 %collective-permute-start.8 = (bf16[4,2,3,48,128]{4,3,2,1,0:T(8,128)(2,1)S(1)}, bf16[4,2,3,48,128]{4,3,2,1,0:T(8,128)(2,1)S(1)}, u32[]{:S(2)}, u32[]{:S(2)}) collective-permute-start(bf16[4,2,3,48,128]{4,3,2,1,0:T(8,128)(2,1)S(1)} %pad_maximum_fusion.2.own_even), channel_id=1, source_target_pairs={{0,6},{1,3},{2,0},{3,5},{4,2},{5,7},{6,4},{7,1},{8,14},{9,11},{10,... | collective-permute-start | bytes 884744 | tf_op jit(solution)/shard_map/ppermute | solution.py:290
  24.8 11.0 %collective-permute-start.7 = (bf16[4,2,3,48,128]{4,3,2,1,0:T(8,128)(2,1)S(1)}, bf16[4,2,3,48,128]{4,3,2,1,0:T(8,128)(2,1)S(1)}, u32[]{:S(2)}, u32[]{:S(2)}) collective-permute-start(bf16[4,2,3,48,128]{4,3,2,1,0:T(8,128)(2,1)S(1)} %pad_maximum_fusion.1.own_odd), channel_id=1, source_target_pairs={{0,2},{1,7},{2,4},{3,1},{4,6},{5,3},{6,0},{7,5},{8,10},{9,15},{10,... | collective-permute-start | bytes 884744 | tf_op jit(solution)/shard_map/ppermute | solution.py:290
  42.3 39.0 %all-to-all-start.1 = ((bf16[8,2,3,48,128]{4,3,2,1,0:T(8,128)(2,1)}), bf16[8,2,3,48,128]{4,3,2,1,0:T(8,128)(2,1)S(1)}, u32[]{:S(2)}, u32[]{:S(2)}) async-start(bf16[8,2,3,48,128]{4,3,2,1,0:T(8,128)(2,1)} %get-tuple-element.33), calls=%async_computation.1 | async-start | bytes 1179648 | tf_op jit(solution)/shard_map/all_to_all | solution.py:350
  46.4 17.8 %collective-permute-start.10 = (bf16[4,2,3,48,128]{4,3,2,1,0:T(8,128)(2,1)S(1)}, bf16[4,2,3,48,128]{4,3,2,1,0:T(8,128)(2,1)S(1)}, u32[]{:S(2)}, u32[]{:S(2)}) collective-permute-start(bf16[4,2,3,48,128]{4,3,2,1,0:T(8,128)(2,1)S(1)} %get-tuple-element.46), channel_id=1, source_target_pairs={{0,2},{2,4},{4,6},{6,0},{1,3},{3,5},{5,7},{7,1},{8,10},{10,12},{12... | collective-permute-start | bytes 884744 | tf_op jit(solution)/shard_map/ppermute | solution.py:280
  46.5 17.7 %collective-permute-start.9 = (bf16[4,2,3,48,128]{4,3,2,1,0:T(8,128)(2,1)S(1)}, bf16[4,2,3,48,128]{4,3,2,1,0:T(8,128)(2,1)S(1)}, u32[]{:S(2)}, u32[]{:S(2)}) collective-permute-start(bf16[4,2,3,48,128]{4,3,2,1,0:T(8,128)(2,1)S(1)} %get-tuple-element.47), channel_id=1, source_target_pairs={{0,6},{2,0},{4,2},{6,4},{1,7},{3,1},{5,3},{7,5},{8,14},{10,8},{12,... | collective-permute-start | bytes 884744 | tf_op jit(solution)/shard_map/ppermute | solution.py:280
  49.7 12.3 %collective-permute-start.11 = (f32[2,12,192]{2,1,0:T(8,128)S(1)}, f32[2,12,192]{2,1,0:T(8,128)S(1)}, u32[]{:S(2)}, u32[]{:S(2)}) collective-permute-start(f32[2,12,192]{2,1,0:T(8,128)S(1)} %get-tuple-element.35), channel_id=1, source_target_pairs={{0,6},{2,0},{4,2},{6,4},{1,7},{3,1},{5,3},{7,5},{8,14},{10,8},{12,... | collective-permute-start | bytes 55304 | tf_op jit(solution)/shard_map/ppermute | solution.py:280
  49.7 14.4 %collective-permute-start.12 = (f32[2,12,192]{2,1,0:T(8,128)S(1)}, f32[2,12,192]{2,1,0:T(8,128)S(1)}, u32[]{:S(2)}, u32[]{:S(2)}) collective-permute-start(f32[2,12,192]{2,1,0:T(8,128)S(1)} %get-tuple-element.35), channel_id=1, source_target_pairs={{0,2},{2,4},{4,6},{6,0},{1,3},{3,5},{5,7},{7,1},{8,10},{10,12},{12... | collective-permute-start | bytes 55304 | tf_op jit(solution)/shard_map/ppermute | solution.py:280
  67.3 5.5 %collective-permute-start.13 = (bf16[2,3,48,128]{3,2,1,0:T(8,128)(2,1)S(1)}, bf16[2,3,48,128]{3,2,1,0:T(8,128)(2,1)S(1)}, u32[]{:S(2)}, u32[]{:S(2)}) collective-permute-start(bf16[2,3,48,128]{3,2,1,0:T(8,128)(2,1)S(1)} %get-tuple-element.37), channel_id=1, source_target_pairs={{0,1},{1,0},{8,9},{9,8},{16,17},{17,16},{24,25},{25,24},{2,3},{3,2... | collective-permute-start | bytes 221192 | tf_op jit(solution)/shard_map/ppermute | solution.py:297
  68.5 6.5 %collective-permute-start.14 = (bf16[2,3,48,128]{3,2,1,0:T(8,128)(2,1)S(1)}, bf16[2,3,48,128]{3,2,1,0:T(8,128)(2,1)S(1)}, u32[]{:S(2)}, u32[]{:S(2)}) collective-permute-start(bf16[2,3,48,128]{3,2,1,0:T(8,128)(2,1)S(1)} %get-tuple-element.38), channel_id=1, source_target_pairs={{0,8},{1,9},{8,0},{9,1},{16,24},{17,25},{24,16},{25,17},{2,10},{3,... | collective-permute-start | bytes 221192 | tf_op jit(solution)/shard_map/ppermute | solution.py:297
  70.3 5.7 %collective-permute-start.15 = (bf16[2,3,48,128]{3,2,1,0:T(8,128)(2,1)S(1)}, bf16[2,3,48,128]{3,2,1,0:T(8,128)(2,1)S(1)}, u32[]{:S(2)}, u32[]{:S(2)}) collective-permute-start(bf16[2,3,48,128]{3,2,1,0:T(8,128)(2,1)S(1)} %get-tuple-element.39), channel_id=1, source_target_pairs={{0,9},{1,8},{8,1},{9,0},{16,25},{17,24},{24,17},{25,16},{2,11},{3,... | collective-permute-start | bytes 221192 | tf_op jit(solution)/shard_map/ppermute | solution.py:297
  70.3 5.7 %collective-permute-start.16 = (bf16[2,3,48,128]{3,2,1,0:T(8,128)(2,1)S(1)}, bf16[2,3,48,128]{3,2,1,0:T(8,128)(2,1)S(1)}, u32[]{:S(2)}, u32[]{:S(2)}) collective-permute-start(bf16[2,3,48,128]{3,2,1,0:T(8,128)(2,1)S(1)} %get-tuple-element.40), channel_id=1, source_target_pairs={{0,16},{1,17},{8,24},{9,25},{16,0},{17,1},{24,8},{25,9},{2,18},{3,... | collective-permute-start | bytes 221192 | tf_op jit(solution)/shard_map/ppermute | solution.py:297
  71.6 4.3 %collective-permute-start.17 = (bf16[2,3,48,128]{3,2,1,0:T(8,128)(2,1)S(1)}, bf16[2,3,48,128]{3,2,1,0:T(8,128)(2,1)S(1)}, u32[]{:S(2)}, u32[]{:S(2)}) collective-permute-start(bf16[2,3,48,128]{3,2,1,0:T(8,128)(2,1)S(1)} %get-tuple-element.41), channel_id=1, source_target_pairs={{0,17},{1,16},{8,25},{9,24},{16,1},{17,0},{24,9},{25,8},{2,19},{3,... | collective-permute-start | bytes 221192 | tf_op jit(solution)/shard_map/ppermute | solution.py:297
  72.8 7.6 %collective-permute-start.18 = (bf16[2,3,48,128]{3,2,1,0:T(8,128)(2,1)S(1)}, bf16[2,3,48,128]{3,2,1,0:T(8,128)(2,1)S(1)}, u32[]{:S(2)}, u32[]{:S(2)}) collective-permute-start(bf16[2,3,48,128]{3,2,1,0:T(8,128)(2,1)S(1)} %get-tuple-element.42), channel_id=1, source_target_pairs={{0,24},{1,25},{8,16},{9,17},{16,8},{17,9},{24,0},{25,1},{2,26},{3,... | collective-permute-start | bytes 221192 | tf_op jit(solution)/shard_map/ppermute | solution.py:297
  75.0 5.4 %collective-permute-start.19 = (bf16[2,3,48,128]{3,2,1,0:T(8,128)(2,1)S(1)}, bf16[2,3,48,128]{3,2,1,0:T(8,128)(2,1)S(1)}, u32[]{:S(2)}, u32[]{:S(2)}) collective-permute-start(bf16[2,3,48,128]{3,2,1,0:T(8,128)(2,1)S(1)} %get-tuple-element.43), channel_id=1, source_target_pairs={{0,25},{1,24},{8,17},{9,16},{16,9},{17,8},{24,1},{25,0},{2,27},{3,... | collective-permute-start | bytes 221192 | tf_op jit(solution)/shard_map/ppermute | solution.py:297
  (3 other events, 16.3 us)
